TPU v7x, 32 devices: a whole 2x2x4 slice. The times are simulated.
32 devices in a mesh: gx: 4 (over y, x), gy: 8 (over z, core).
Axes of the slice: x: 2, y: 2, z: 4, core: 2. Of those that a mesh axis runs over, the one named last changes fastest.
Arguments:
- traveltime: float32 [8, 32, 64, 512], P(None, None, 'gy', 'gx'), may hold values from 1 to 4
- adjoint_start: float32 [8, 32, 64, 512], P(None, None, 'gy', 'gx'), may hold values from -6 to 6
- upwind_flags: int32 [8, 32, 64, 512], P(None, None, 'gy', 'gx'), may hold values from 0 to 7, as said below
- slowness: float32 [32, 64, 512], P(None, 'gy', 'gx'), may hold values from 0.15 to 0.6
- residual_rows: float32 [2048, 8], P(('gx', 'gy')), may hold values from -6 to 6
- station_tile: int32 [2048, 1], P(('gx', 'gy')), may hold values from 0 to 31; in each aligned block of 64 rows (0 to 63, 64 to 127, ...) at most 4 rows name the same one
- station_cell: int32 [2048], P(('gx', 'gy')), may hold values from 0 to 32767
Outputs:
- adjoint: float32 [8, 32, 64, 512], P(None, None, 'gy', 'gx')
- gradient: float32 [32, 64, 512], P(None, 'gy', 'gx')
Inputs may be any that keep to these rules, and one draw needn't show every extreme that they name: `upwind_flags`: bit k of a cell's value is 1 where its upwind neighbour along x, y, z (k = 0, 1, 2) lies at the higher index; at every face of the grid the upwind neighbour lies inside the grid. `station_tile`: among the records of one device no tile is named more than 4 times, a bound that some block reaches.
All inputs are finite; a program needn't handle non-finite values.
Results may differ from a plain program's by a relative error of at most 0.00002.
Values sent between devices are 32-bit elements; how exact they have to be, the bound alone decides.
A program may use at most 128 MiB of HBM per device.

v0:
```python
import jax
import jax.numpy as jnp
from jax import lax
from jax.sharding import PartitionSpec as P

SWEEPS = 3
CAP = 4


def with_halo(cells, sides, width):
    for axis, dim in sides:
        count = lax.axis_size(axis)
        ends = count - 1
        head = lax.slice_in_dim(cells, 0, width, axis=dim)
        tail = lax.slice_in_dim(cells, cells.shape[dim] - width, cells.shape[dim], axis=dim)
        cells = jnp.concatenate(
            [
                lax.ppermute(tail, axis, [(i, (i + 1) % count) for i in range(ends)]),
                cells,
                lax.ppermute(head, axis, [((i + 1) % count, i) for i in range(ends)]),
            ],
            axis=dim,
        )
    return cells


def hpad(values):
    widths = [(0, 0)] * (values.ndim - 2) + [(1, 1), (1, 1)]
    return jnp.pad(values, widths)


def relax(adjoint, push_x, push_y, push_z, source, denominator):
    plus_x = jnp.maximum(push_x, 0.0) * adjoint
    minus_x = jnp.maximum(-push_x, 0.0) * adjoint
    plus_y = jnp.maximum(push_y, 0.0) * adjoint
    minus_y = jnp.maximum(-push_y, 0.0) * adjoint
    plus_z = jnp.pad(jnp.maximum(push_z, 0.0) * adjoint, ((0, 0), (1, 1), (0, 0), (0, 0)))
    minus_z = jnp.pad(jnp.maximum(-push_z, 0.0) * adjoint, ((0, 0), (1, 1), (0, 0), (0, 0)))
    inflow = (
        plus_x[:, :, 1:-1, :-2]
        + minus_x[:, :, 1:-1, 2:]
        + plus_y[:, :, :-2, 1:-1]
        + minus_y[:, :, 2:, 1:-1]
    )
    vertical = plus_z[:, :-2] + minus_z[:, 2:]
    inflow = inflow + vertical[:, :, 1:-1, 1:-1]
    return (source[:, :, 1:-1, 1:-1] + inflow) / denominator[:, :, 1:-1, 1:-1]


def smooth(extended):
    centre = extended[:, 1:-1, 1:-1]
    beside = (
        extended[:, 1:-1, 2:]
        + extended[:, 1:-1, :-2]
        + extended[:, 2:, 1:-1]
        + extended[:, :-2, 1:-1]
    )
    return centre + 0.125 * (beside - 4.0 * centre)


def shards(
    traveltime, adjoint_start, upwind_flags, slowness, residual_rows, station_tile, station_cell
):
    sources, levels, width_y, width_x = traveltime.shape
    cell_count = levels * width_y * width_x
    devices = lax.axis_size(("gx", "gy"))
    capacity = CAP
    tiles = station_tile[:, 0]
    onehot = (tiles[:, None] == jnp.arange(devices, dtype=jnp.int32)[None, :]).astype(jnp.int32)
    before = jnp.cumsum(onehot, axis=0) - onehot
    slot_rank = jnp.sum(before * onehot, axis=1)
    position = tiles * capacity + slot_rank
    rows_out = jax.ops.segment_sum(residual_rows, position, num_segments=devices * capacity)
    cells_out = (
        jax.ops.segment_sum(
            station_cell.astype(jnp.float32) + 1.0, position, num_segments=devices * capacity
        )
        - 1.0
    )
    rows_in, cells_in = (
        lax.all_to_all(
            rows_out.reshape(devices, capacity, sources),
            ("gx", "gy"),
            split_axis=0,
            concat_axis=0,
            tiled=True,
        ),
        lax.all_to_all(
            cells_out.reshape(devices, capacity),
            ("gx", "gy"),
            split_axis=0,
            concat_axis=0,
            tiled=True,
        ),
    )
    rows_in = rows_in.reshape(-1, sources)
    cells_in = cells_in.reshape(-1)
    target = jnp.where(cells_in >= 0.0, cells_in.astype(jnp.int32), cell_count)
    source = jnp.zeros((sources, cell_count), jnp.float32)
    source = (
        source.at[:, target].add(rows_in.T, mode="drop").reshape(sources, levels, width_y, width_x)
    )
    extended = with_halo(traveltime, (("gx", 3), ("gy", 2)), 1)
    padded_z = jnp.pad(traveltime, ((0, 0), (1, 1), (0, 0), (0, 0)))
    plus_x = upwind_flags % 2 == 1
    plus_y = upwind_flags // 2 % 2 == 1
    plus_z = upwind_flags // 4 == 1
    up_x = jnp.where(plus_x, extended[:, :, 1:-1, 2:], extended[:, :, 1:-1, :-2])
    up_y = jnp.where(plus_y, extended[:, :, 2:, 1:-1], extended[:, :, :-2, 1:-1])
    up_z = jnp.where(plus_z, padded_z[:, 2:], padded_z[:, :-2])
    coef_x = jnp.maximum(traveltime - up_x, 0.0)
    coef_y = jnp.maximum(traveltime - up_y, 0.0)
    coef_z = jnp.maximum(traveltime - up_z, 0.0)
    push_x = jnp.where(plus_x, coef_x, -coef_x)
    push_y = jnp.where(plus_y, coef_y, -coef_y)
    push_z = jnp.where(plus_z, coef_z, -coef_z)
    denominator = hpad(1.0 + coef_x + coef_y + coef_z)
    pushes = with_halo(jnp.stack([push_x, push_y]), (("gx", 4), ("gy", 3)), 1)
    push_vertical = hpad(push_z)
    source_wide = hpad(source)
    adjoint = adjoint_start
    for repeat in range(SWEEPS):
        adjoint_wide = with_halo(adjoint, (("gx", 3), ("gy", 2)), 1)
        adjoint = relax(adjoint_wide, pushes[0], pushes[1], push_vertical, source_wide, denominator)
    total = jnp.sum(adjoint, axis=0)
    total_wide = with_halo(total, (("gx", 2), ("gy", 1)), 1)
    gradient = slowness * smooth(total_wide)
    return (adjoint, gradient)


def solution(mesh):
    placed = (
        P(None, None, "gy", "gx"),
        P(None, None, "gy", "gx"),
        P(None, None, "gy", "gx"),
        P(None, "gy", "gx"),
        P(("gx", "gy"), None),
        P(("gx", "gy"), None),
        P(("gx", "gy")),
    )
    return jax.shard_map(
        shards,
        mesh=mesh,
        in_specs=placed,
        out_specs=(P(None, None, "gy", "gx"), P(None, "gy", "gx")),
        check_vma=False,
    )
```

profile of v0, /device:TPU:5, one launch (start us, length us, event | category | flops | bytes accessed | tf_op | source)
XLA Modules:
  0.0 229.1 jit_solution(959943840858501557)
XLA Ops:
  5.3 6.4 %all-to-all-start = ((f32[32,1,4]{2,1,0:T(1,128)}), f32[32,1,4]{2,1,0:T(1,128)S(1)}, u32[]{:S(2)}, u32[]{:S(2)}) async-start(f32[32,1,4]{2,1,0:T(1,128)} %bitcast.3), calls=%async_computation | async-start | bytes 32768 | tf_op jit(solution)/shard_map/all_to_all | solution.py:88
  11.7 2.0 fusion.64
  14.2 3.1 %collective-permute-start.1 = (f32[8,32,8,1]{1,2,3,0:T(8,128)S(1)}, f32[8,32,8,1]{1,2,3,0:T(8,128)S(1)}, u32[]{:S(2)}, u32[]{:S(2)}) collective-permute-start(f32[8,32,8,1]{1,2,3,0:T(8,128)S(1)} %copy.266), channel_id=1, source_target_pairs={{0,8},{8,16},{16,24},{1,9},{9,17},{17,25},{2,10},{10,18},{18,26},{... | collective-permute-start | bytes 24584 | tf_op jit(solution)/shard_map/ppermute | solution.py:18
  17.7 3.2 %collective-permute-start = (f32[8,32,8,1]{1,2,3,0:T(8,128)S(1)}, f32[8,32,8,1]{1,2,3,0:T(8,128)S(1)}, u32[]{:S(2)}, u32[]{:S(2)}) collective-permute-start(f32[8,32,8,1]{1,2,3,0:T(8,128)S(1)} %copy.265), channel_id=1, source_target_pairs={{8,0},{16,8},{24,16},{9,1},{17,9},{25,17},{10,2},{18,10},{26,18},{... | collective-permute-start | bytes 24584 | tf_op jit(solution)/shard_map/ppermute | solution.py:20
  23.9 2.2 collective-permute-start.9
  27.2 3.1 %collective-permute-start.8 = (f32[8,32,8,1]{1,2,3,0:T(8,128)}, f32[8,32,8,1]{1,2,3,0:T(8,128)}, u32[]{:S(2)}, u32[]{:S(2)}) collective-permute-start(f32[8,32,8,1]{1,2,3,0:T(8,128)} %copy.267), channel_id=1, source_target_pairs={{0,8},{8,16},{16,24},{1,9},{9,17},{17,25},{2,10},{10,18},{18,26},{... | collective-permute-start | bytes 24584 | tf_op jit(solution)/shard_map/ppermute | solution.py:18
  33.3 6.0 %all-to-all-start.1 = ((f32[32,4,8]{2,1,0:T(4,128)}), f32[32,4,8]{2,1,0:T(4,128)S(1)}, u32[]{:S(2)}, u32[]{:S(2)}) async-start(f32[32,4,8]{2,1,0:T(4,128)} %bitcast.5), calls=%async_computation.1 | async-start | bytes 131072 | tf_op jit(solution)/shard_map/all_to_all | solution.py:81
  41.7 3.4 %collective-permute-start.3 = (f32[8,32,1,130]{3,1,2,0:T(8,128)}, f32[8,32,1,130]{3,1,2,0:T(8,128)S(1)}, u32[]{:S(2)}, u32[]{:S(2)}) collective-permute-start(f32[8,32,1,130]{3,1,2,0:T(8,128)} %get-tuple-element.33), channel_id=1, source_target_pairs={{0,1},{1,2},{2,3},{3,4},{4,5},{5,6},{6,7},{8,9},{9,10},{10,11},{11... | collective-permute-start | bytes 399368 | tf_op jit(solution)/shard_map/ppermute | solution.py:18
  45.0 1.9 collective-permute-start.2
  47.0 7.8 %scatter_custom_fusion.2 = f32[8,32768]{0,1:T(8,128)} fusion(s32[128]{0:T(128)S(1)} %fusion.56, f32[128,8]{1,0:T(8,128)S(1)} %bitcast.26, f32[]{:T(128)} %constant.59.clone.1), kind=kCustom, calls=%fused_computation.3 | custom fusion | flops 1024 | bytes 1048580 | tf_op jit(solution)/shard_map/scatter-add | solution.py:101
  54.8 10.6 %copy.259 = f32[8,32,8,128]{3,1,2,0:T(8,128)} copy(f32[8,32,8,128]{0,3,2,1:T(8,128)} %bitcast.25) | data formatting | bytes 2097152 | tf_op jit(solution)/shard_map/reshape | solution.py:101
  66.9 2.2 copy.244
  69.1 2.2 pad_maximum_fusion.34
  71.4 1.9 collective-permute-start.11
  73.3 3.6 %collective-permute-start.10 = (f32[8,32,1,130]{3,1,2,0:T(8,128)}, f32[8,32,1,130]{3,1,2,0:T(8,128)}, u32[]{:S(2)}, u32[]{:S(2)}) collective-permute-start(f32[8,32,1,130]{3,1,2,0:T(8,128)} %get-tuple-element.34), channel_id=1, source_target_pairs={{0,1},{1,2},{2,3},{3,4},{4,5},{5,6},{6,7},{8,9},{9,10},{10,11},{11... | collective-permute-start | bytes 399368 | tf_op jit(solution)/shard_map/ppermute | solution.py:18
  77.0 4.1 %fusion.13 = (f32[1,8,32,8,128]{4,2,3,1,0:T(8,128)S(1)}, f32[1,8,32,8,128]{4,2,3,1,0:T(8,128)S(1)}, f32[8,32,8,128]{3,1,2,0:T(8,128)S(1)}) fusion(f32[8,32,8,128]{3,1,2,0:T(8,128)S(1)} %copy.232, f32[8,32,8,1]{3,1,2,0:T(8,128)S(1)} %copy.230, f32[8,32,8,1]{3,1,2,0:T(8,128)} %copy-done.6, s32[8,32,8,128]{3,2,1,0:T(8,128)S(1)} %copy-done.28, ...), kind=kLoop, calls=%fused_computation.50 | loop fusion | flops 17301504 | bytes 5525504 | tf_op jit(solution)/shard_map/stack | solution.py:118
  81.2 2.8 %slice_maximum_fusion = (f32[2,8,32,8,1]{4,2,3,1,0:T(8,128)}, f32[2,8,32,8,1]{4,2,3,1,0:T(8,128)}) fusion(f32[1,8,32,8,128]{4,2,3,1,0:T(8,128)S(1)} %get-tuple-element.27, f32[1,8,32,8,128]{4,2,3,1,0:T(8,128)S(1)} %get-tuple-element.26), kind=kLoop, calls=%fused_computation.29 | loop fusion | flops 8192 | bytes 2129920 | tf_op jit(solution)/shard_map/stack | solution.py:118
  83.9 2.5 %copy.239 = f32[2,8,32,8,1]{2,3,4,1,0:T(8,128)S(1)} copy(f32[2,8,32,8,1]{4,2,3,1,0:T(8,128)} %get-tuple-element.37) | data formatting | bytes 32768 | tf_op jit(solution)/shard_map/slice | solution.py:14
  86.5 3.3 %collective-permute-start.5 = (f32[2,8,32,8,1]{2,3,4,1,0:T(8,128)S(1)}, f32[2,8,32,8,1]{2,3,4,1,0:T(8,128)S(1)}, u32[]{:S(2)}, u32[]{:S(2)}) collective-permute-start(f32[2,8,32,8,1]{2,3,4,1,0:T(8,128)S(1)} %copy.239), channel_id=1, source_target_pairs={{8,0},{16,8},{24,16},{9,1},{17,9},{25,17},{10,2},{18,10},{26,18},{... | collective-permute-start | bytes 49160 | tf_op jit(solution)/shard_map/ppermute | solution.py:20
  89.7 3.0 %copy.238 = f32[2,8,32,8,1]{2,3,4,1,0:T(8,128)} copy(f32[2,8,32,8,1]{4,2,3,1,0:T(8,128)} %get-tuple-element.36) | data formatting | bytes 32768 | tf_op jit(solution)/shard_map/slice | solution.py:15
  92.8 2.2 collective-permute-start.4
  95.0 5.1 %fusion.4 = (f32[8,32,10,130]{3,1,2,0:T(8,128)}, f32[8,32,10,130]{3,1,2,0:T(8,128)}) fusion(f32[8,32,8,128]{3,1,2,0:T(8,128)S(1)} %get-tuple-element.38, f32[8,32,1,130]{3,1,2,0:T(8,128)} %collective-permute-done.11, f32[8,32,8,1]{3,1,2,0:T(8,128)S(1)} %copy-done.19, f32[8,32,8,128]{3,1,2,0:T(8,128)S(1)} %copy-done.18, f32[8,32,8,1]{3,1,2,0:T(8,128)} %copy.244, ...), kind=kLoop, calls=%fused_computation.16 | loop fusion | flops 1996800 | bytes 5042176 | tf_op jit(solution)/shard_map/mul | solution.py:37
  100.9 3.0 %copy.240 = f32[2,8,32,8,1]{4,2,3,1,0:T(8,128)} copy(f32[2,8,32,8,1]{2,3,4,1,0:T(8,128)} %collective-permute-done.4) | data formatting | bytes 32768 | tf_op jit(solution)/shard_map/ppermute | solution.py:18
  105.8 1.9 collective-permute-start.7
  107.7 3.6 %collective-permute-start.6 = (f32[2,8,32,1,130]{4,2,3,1,0:T(8,128)S(1)}, f32[2,8,32,1,130]{4,2,3,1,0:T(8,128)S(1)}, u32[]{:S(2)}, u32[]{:S(2)}) collective-permute-start(f32[2,8,32,1,130]{4,2,3,1,0:T(8,128)S(1)} %get-tuple-element.20), channel_id=1, source_target_pairs={{0,1},{1,2},{2,3},{3,4},{4,5},{5,6},{6,7},{8,9},{9,10},{10,11},{11... | collective-permute-start | bytes 798728 | tf_op jit(solution)/shard_map/ppermute | solution.py:18
  113.1 3.2 %pad_slice_fusion.4 = (f32[8,32,10,130]{3,1,2,0:T(8,128)}, f32[8,32,10,130]{3,1,2,0:T(8,128)}) fusion(f32[8,32,10,130]{3,1,2,0:T(8,128)S(1)} %fusion.8, f32[8,32,10,130]{3,1,2,0:T(8,128)S(1)} %copy-done.16), kind=kLoop, calls=%fused_computation.10 | loop fusion | bytes 5324800 | tf_op jit(solution)/shard_map/slice | solution.py:45
  117.5 2.5 %pad_maximum_fusion = f32[2,8,32,10,130]{4,2,3,1,0:T(8,128)S(1)} fusion(f32[2,8,32,1,130]{4,2,3,1,0:T(8,128)S(1)} %collective-permute-done.7, f32[2,8,32,8,1]{4,2,3,1,0:T(8,128)S(1)} %copy.241, f32[1,8,32,8,128]{4,2,3,1,0:T(8,128)S(1)} %copy-done.11, f32[1,8,32,8,128]{4,2,3,1,0:T(8,128)S(1)} %copy-done.9, f32[2,8,32,8,1]{4,2,3,1,0:T(8,128)S(1)} %copy-done.1, ...), kind=kLoop, calls=%fused_computation.5 | loop fusion | flops 3328000 | bytes 5324800 | tf_op jit(solution)/shard_map/concatenate | solution.py:16
  120.0 2.6 %maximum_bitcast_fusion.2 = (f32[8,32,10,130]{3,1,2,0:T(8,128)S(1)}, f32[8,32,10,130]{3,1,2,0:T(8,128)S(1)}, f32[8,32,10,130]{3,1,2,0:T(8,128)S(1)}, f32[8,32,10,130]{3,1,2,0:T(8,128)}) fusion(f32[2,8,32,10,130]{4,2,3,1,0:T(8,128)S(1)} %pad_maximum_fusion), kind=kLoop, calls=%fused_computation.26 | loop fusion | flops 1996800 | bytes 7987200 | tf_op jit(solution)/shard_map/max | solution.py:34
  123.4 8.4 %fusion.33 = (f32[8,32,8,128]{3,1,2,0:T(8,128)S(1)}, f32[8,32,8,128]{3,1,2,0:T(8,128)}) fusion(f32[8,32,8,128]{3,1,2,0:T(8,128)S(1)} %copy-done.12, f32[8,32,10,130]{3,1,2,0:T(8,128)} %get-tuple-element.51, f32[8,32,10,130]{3,1,2,0:T(8,128)} %get-tuple-element.52, f32[8,32,10,130]{3,1,2,0:T(8,128)S(1)} %copy-done, f32[8,32,10,130]{3,1,2,0:T(8,128)} %get-tuple-element.25, ...), kind=kLoop, calls=%fused_computation.81 | loop fusion | flops 19398656 | bytes 16011264 | tf_op jit(solution)/shard_map/div | solution.py:47
  135.2 4.0 %collective-permute-start.13 = (f32[8,32,8,1]{1,2,3,0:T(8,128)S(1)}, f32[8,32,8,1]{1,2,3,0:T(8,128)S(1)}, u32[]{:S(2)}, u32[]{:S(2)}) collective-permute-start(f32[8,32,8,1]{1,2,3,0:T(8,128)S(1)} %copy.251), channel_id=1, source_target_pairs={{8,0},{16,8},{24,16},{9,1},{17,9},{25,17},{10,2},{18,10},{26,18},{... | collective-permute-start | bytes 24584 | tf_op jit(solution)/shard_map/ppermute | solution.py:20
  140.9 1.9 collective-permute-start.12
  144.2 2.2 collective-permute-done.12
  149.4 1.9 collective-permute-start.15
  151.4 6.1 %collective-permute-start.14 = (f32[8,32,1,130]{3,1,2,0:T(8,128)S(1)}, f32[8,32,1,130]{3,1,2,0:T(8,128)S(1)}, u32[]{:S(2)}, u32[]{:S(2)}) collective-permute-start(f32[8,32,1,130]{3,1,2,0:T(8,128)S(1)} %get-tuple-element.30), channel_id=1, source_target_pairs={{0,1},{1,2},{2,3},{3,4},{4,5},{5,6},{6,7},{8,9},{9,10},{10,11},{11... | collective-permute-start | bytes 399368 | tf_op jit(solution)/shard_map/ppermute | solution.py:18
  157.4 1.9 collective-permute-done.15
  162.7 2.0 pad_slice_fusion.2
  165.9 6.0 %fusion.27 = f32[8,32,8,128]{3,1,2,0:T(8,128)S(1)} fusion(f32[8,32,8,128]{3,1,2,0:T(8,128)S(1)} %copy-done.26, f32[8,32,8,128]{3,1,2,0:T(8,128)S(1)} %copy-done.12, f32[8,32,10,130]{3,1,2,0:T(8,128)} %pad_slice_fusion.2, f32[8,32,10,130]{3,1,2,0:T(8,128)S(1)} %pad_slice_fusion.3, f32[8,32,10,130]{3,1,2,0:T(8,128)S(1)} %get-tuple-element.15, ...), kind=kLoop, calls=%fused_computation.70 | loop fusion | flops 2883584 | bytes 13631488 | tf_op jit(solution)/shard_map/div | solution.py:47
  175.4 1.9 collective-permute-start.17
  179.0 3.4 %collective-permute-start.16 = (f32[8,32,8,1]{1,2,3,0:T(8,128)S(1)}, f32[8,32,8,1]{1,2,3,0:T(8,128)S(1)}, u32[]{:S(2)}, u32[]{:S(2)}) collective-permute-start(f32[8,32,8,1]{1,2,3,0:T(8,128)S(1)} %copy.255), channel_id=1, source_target_pairs={{0,8},{8,16},{16,24},{1,9},{9,17},{17,25},{2,10},{10,18},{18,26},{... | collective-permute-start | bytes 24584 | tf_op jit(solution)/shard_map/ppermute | solution.py:18
  187.5 1.9 collective-permute-start.19
  189.5 5.5 %collective-permute-start.18 = (f32[8,32,1,130]{3,1,2,0:T(8,128)S(1)}, f32[8,32,1,130]{3,1,2,0:T(8,128)S(1)}, u32[]{:S(2)}, u32[]{:S(2)}) collective-permute-start(f32[8,32,1,130]{3,1,2,0:T(8,128)S(1)} %get-tuple-element.28), channel_id=1, source_target_pairs={{0,1},{1,2},{2,3},{3,4},{4,5},{5,6},{6,7},{8,9},{9,10},{10,11},{11... | collective-permute-start | bytes 399368 | tf_op jit(solution)/shard_map/ppermute | solution.py:18
  195.0 2.1 collective-permute-done.19
  200.9 2.2 pad_slice_fusion.1
  203.2 6.0 %fusion.60 = (f32[32,8,128]{2,0,1:T(8,128)S(1)}, f32[8,32,8,128]{3,1,2,0:T(8,128)S(1)}) fusion(f32[8,32,8,128]{3,1,2,0:T(8,128)S(1)} %copy-done.27, f32[8,32,8,128]{3,1,2,0:T(8,128)S(1)} %copy-done.12, f32[8,32,10,130]{3,1,2,0:T(8,128)S(1)} %pad_slice_fusion, f32[8,32,10,130]{3,1,2,0:T(8,128)} %pad_slice_fusion.1, ...), kind=kLoop, calls=%fused_computation.155 | loop fusion | flops 3112960 | bytes 13762560 | tf_op jit(solution)/shard_map/reduce_sum | solution.py:125
  209.4 1.9 collective-permute-start.20
  211.3 3.4 %collective-permute-start.21 = (f32[32,8,1]{0,1,2:T(8,128)S(1)}, f32[32,8,1]{0,1,2:T(8,128)S(1)}, u32[]{:S(2)}, u32[]{:S(2)}) collective-permute-start(f32[32,8,1]{0,1,2:T(8,128)S(1)} %get-tuple-element.49), channel_id=1, source_target_pairs={{0,8},{8,16},{16,24},{1,9},{9,17},{17,25},{2,10},{10,18},{18,26},{... | collective-permute-start | bytes 3080 | tf_op jit(solution)/shard_map/ppermute | solution.py:18
  216.7 5.5 %collective-permute-start.23 = (f32[32,1,130]{0,1,2:T(1,128)S(1)}, f32[32,1,130]{0,1,2:T(1,128)S(1)}, u32[]{:S(2)}, u32[]{:S(2)}) collective-permute-start(f32[32,1,130]{0,1,2:T(1,128)S(1)} %get-tuple-element.48), channel_id=1, source_target_pairs={{0,1},{1,2},{2,3},{3,4},{4,5},{5,6},{6,7},{8,9},{9,10},{10,11},{11... | collective-permute-start | bytes 49928 | tf_op jit(solution)/shard_map/ppermute | solution.py:18
  222.2 1.9 collective-permute-start.22
  (138 shorter events, 58.0 us)
Async XLA Ops:
  5.3 28.0 %all-to-all-start = ((f32[32,1,4]{2,1,0:T(1,128)}), f32[32,1,4]{2,1,0:T(1,128)S(1)}, u32[]{:S(2)}, u32[]{:S(2)}) async-start(f32[32,1,4]{2,1,0:T(1,128)} %bitcast.3), calls=%async_computation | async-start | bytes 32768 | tf_op jit(solution)/shard_map/all_to_all | solution.py:88
  11.7 9.2 %copy-start.25 = (f32[8,32,8,128]{3,2,1,0:T(8,128)S(1)}, f32[8,32,8,128]{3,2,1,0:T(8,128)}, u32[]{:S(2)}) copy-start(f32[8,32,8,128]{3,2,1,0:T(8,128)} %param.8) | copy-start | bytes 3145732
  14.2 25.4 %collective-permute-start.1 = (f32[8,32,8,1]{1,2,3,0:T(8,128)S(1)}, f32[8,32,8,1]{1,2,3,0:T(8,128)S(1)}, u32[]{:S(2)}, u32[]{:S(2)}) collective-permute-start(f32[8,32,8,1]{1,2,3,0:T(8,128)S(1)} %copy.266), channel_id=1, source_target_pairs={{0,8},{8,16},{16,24},{1,9},{9,17},{17,25},{2,10},{10,18},{18,26},{... | collective-permute-start | bytes 24584 | tf_op jit(solution)/shard_map/ppermute | solution.py:18
  17.7 12.5 %copy-start.24 = (f32[8,32,8,128]{3,2,1,0:T(8,128)S(1)}, f32[8,32,8,128]{3,2,1,0:T(8,128)}, u32[]{:S(2)}) copy-start(f32[8,32,8,128]{3,2,1,0:T(8,128)} %param.7) | copy-start | bytes 3145732
  17.7 22.3 %collective-permute-start = (f32[8,32,8,1]{1,2,3,0:T(8,128)S(1)}, f32[8,32,8,1]{1,2,3,0:T(8,128)S(1)}, u32[]{:S(2)}, u32[]{:S(2)}) collective-permute-start(f32[8,32,8,1]{1,2,3,0:T(8,128)S(1)} %copy.265), channel_id=1, source_target_pairs={{8,0},{16,8},{24,16},{9,1},{17,9},{25,17},{10,2},{18,10},{26,18},{... | collective-permute-start | bytes 24584 | tf_op jit(solution)/shard_map/ppermute | solution.py:20
  23.9 41.5 %collective-permute-start.9 = (f32[8,32,8,1]{1,2,3,0:T(8,128)S(1)}, f32[8,32,8,1]{1,2,3,0:T(8,128)S(1)}, u32[]{:S(2)}, u32[]{:S(2)}) collective-permute-start(f32[8,32,8,1]{1,2,3,0:T(8,128)S(1)} %copy.268), channel_id=1, source_target_pairs={{8,0},{16,8},{24,16},{9,1},{17,9},{25,17},{10,2},{18,10},{26,18},{... | collective-permute-start | bytes 24584 | tf_op jit(solution)/shard_map/ppermute | solution.py:20
  26.1 5.8 %copy-start.31 = (f32[64,8]{0,1:T(8,128)S(1)}, f32[64,8]{0,1:T(8,128)}, u32[]{:S(2)}) copy-start(f32[64,8]{0,1:T(8,128)} %param.11) | copy-start | bytes 6148
  27.2 39.8 %collective-permute-start.8 = (f32[8,32,8,1]{1,2,3,0:T(8,128)}, f32[8,32,8,1]{1,2,3,0:T(8,128)}, u32[]{:S(2)}, u32[]{:S(2)}) collective-permute-start(f32[8,32,8,1]{1,2,3,0:T(8,128)} %copy.267), channel_id=1, source_target_pairs={{0,8},{8,16},{16,24},{1,9},{9,17},{17,25},{2,10},{10,18},{18,26},{... | collective-permute-start | bytes 24584 | tf_op jit(solution)/shard_map/ppermute | solution.py:18
  30.5 46.5 %copy-start.2 = (f32[8,32,8,128]{3,1,2,0:T(8,128)}, f32[8,32,8,128]{3,1,2,0:T(8,128)S(1)}, u32[]{:S(2)}) copy-start(f32[8,32,8,128]{3,1,2,0:T(8,128)S(1)} %copy.232) | copy-start | bytes 3145732
  33.3 13.7 %all-to-all-start.1 = ((f32[32,4,8]{2,1,0:T(4,128)}), f32[32,4,8]{2,1,0:T(4,128)S(1)}, u32[]{:S(2)}, u32[]{:S(2)}) async-start(f32[32,4,8]{2,1,0:T(4,128)} %bitcast.5), calls=%async_computation.1 | async-start | bytes 131072 | tf_op jit(solution)/shard_map/all_to_all | solution.py:81
  40.0 36.9 %copy-start.4 = (f32[8,32,8,1]{3,1,2,0:T(8,128)}, f32[8,32,8,1]{3,1,2,0:T(8,128)S(1)}, u32[]{:S(2)}) copy-start(f32[8,32,8,1]{3,1,2,0:T(8,128)S(1)} %copy.230) | copy-start | bytes 24580
  40.5 14.3 %copy-start.6 = (f32[8,32,8,1]{3,1,2,0:T(8,128)}, f32[8,32,8,1]{3,1,2,0:T(8,128)S(1)}, u32[]{:S(2)}) copy-start(f32[8,32,8,1]{3,1,2,0:T(8,128)S(1)} %copy.228) | copy-start | bytes 24580
  41.7 35.3 %collective-permute-start.3 = (f32[8,32,1,130]{3,1,2,0:T(8,128)}, f32[8,32,1,130]{3,1,2,0:T(8,128)S(1)}, u32[]{:S(2)}, u32[]{:S(2)}) collective-permute-start(f32[8,32,1,130]{3,1,2,0:T(8,128)} %get-tuple-element.33), channel_id=1, source_target_pairs={{0,1},{1,2},{2,3},{3,4},{4,5},{5,6},{6,7},{8,9},{9,10},{10,11},{11... | collective-permute-start | bytes 399368 | tf_op jit(solution)/shard_map/ppermute | solution.py:18
  45.0 31.9 %collective-permute-start.2 = (f32[8,32,1,130]{3,1,2,0:T(8,128)}, f32[8,32,1,130]{3,1,2,0:T(8,128)}, u32[]{:S(2)}, u32[]{:S(2)}) collective-permute-start(f32[8,32,1,130]{3,1,2,0:T(8,128)} %get-tuple-element.32), channel_id=1, source_target_pairs={{1,0},{2,1},{3,2},{4,3},{5,4},{6,5},{7,6},{9,8},{10,9},{11,10},{12... | collective-permute-start | bytes 399368 | tf_op jit(solution)/shard_map/ppermute | solution.py:20
  65.4 3.7 %copy-start.17 = (f32[8,32,8,128]{3,1,2,0:T(8,128)S(1)}, f32[8,32,8,128]{3,1,2,0:T(8,128)}, u32[]{:S(2)}) copy-start(f32[8,32,8,128]{3,1,2,0:T(8,128)} %copy.245) | copy-start | bytes 3145732
  69.1 7.9 %copy-start.28 = (s32[8,32,8,128]{3,2,1,0:T(8,128)S(1)}, s32[8,32,8,128]{3,2,1,0:T(8,128)}, u32[]{:S(2)}) copy-start(s32[8,32,8,128]{3,2,1,0:T(8,128)} %param.9) | copy-start | bytes 3145732
  71.4 23.6 %collective-permute-start.11 = (f32[8,32,1,130]{3,1,2,0:T(8,128)}, f32[8,32,1,130]{3,1,2,0:T(8,128)}, u32[]{:S(2)}, u32[]{:S(2)}) collective-permute-start(f32[8,32,1,130]{3,1,2,0:T(8,128)} %get-tuple-element.35), channel_id=1, source_target_pairs={{1,0},{2,1},{3,2},{4,3},{5,4},{6,5},{7,6},{9,8},{10,9},{11,10},{12... | collective-permute-start | bytes 399368 | tf_op jit(solution)/shard_map/ppermute | solution.py:20
  73.3 21.7 %collective-permute-start.10 = (f32[8,32,1,130]{3,1,2,0:T(8,128)}, f32[8,32,1,130]{3,1,2,0:T(8,128)}, u32[]{:S(2)}, u32[]{:S(2)}) collective-permute-start(f32[8,32,1,130]{3,1,2,0:T(8,128)} %get-tuple-element.34), channel_id=1, source_target_pairs={{0,1},{1,2},{2,3},{3,4},{4,5},{5,6},{6,7},{8,9},{9,10},{10,11},{11... | collective-permute-start | bytes 399368 | tf_op jit(solution)/shard_map/ppermute | solution.py:18
  83.9 11.1 %copy-start.18 = (f32[8,32,8,128]{3,1,2,0:T(8,128)S(1)}, f32[8,32,8,128]{3,1,2,0:T(8,128)}, u32[]{:S(2)}) copy-start(f32[8,32,8,128]{3,1,2,0:T(8,128)} %copy.245) | copy-start | bytes 3145732
  83.9 11.1 %copy-start.19 = (f32[8,32,8,1]{3,1,2,0:T(8,128)S(1)}, f32[8,32,8,1]{3,1,2,0:T(8,128)}, u32[]{:S(2)}) copy-start(f32[8,32,8,1]{3,1,2,0:T(8,128)} %copy.246) | copy-start | bytes 24580
  86.5 13.6 %collective-permute-start.5 = (f32[2,8,32,8,1]{2,3,4,1,0:T(8,128)S(1)}, f32[2,8,32,8,1]{2,3,4,1,0:T(8,128)S(1)}, u32[]{:S(2)}, u32[]{:S(2)}) collective-permute-start(f32[2,8,32,8,1]{2,3,4,1,0:T(8,128)S(1)} %copy.239), channel_id=1, source_target_pairs={{8,0},{16,8},{24,16},{9,1},{17,9},{25,17},{10,2},{18,10},{26,18},{... | collective-permute-start | bytes 49160 | tf_op jit(solution)/shard_map/ppermute | solution.py:20
  92.8 8.2 %collective-permute-start.4 = (f32[2,8,32,8,1]{2,3,4,1,0:T(8,128)}, f32[2,8,32,8,1]{2,3,4,1,0:T(8,128)}, u32[]{:S(2)}, u32[]{:S(2)}) collective-permute-start(f32[2,8,32,8,1]{2,3,4,1,0:T(8,128)} %copy.238), channel_id=1, source_target_pairs={{0,8},{8,16},{16,24},{1,9},{9,17},{17,25},{2,10},{10,18},{18,26},{... | collective-permute-start | bytes 49160 | tf_op jit(solution)/shard_map/ppermute | solution.py:18
  103.9 7.4 %copy-start = (f32[8,32,10,130]{3,1,2,0:T(8,128)S(1)}, f32[8,32,10,130]{3,1,2,0:T(8,128)}, u32[]{:S(2)}) copy-start(f32[8,32,10,130]{3,1,2,0:T(8,128)} %get-tuple-element.19) | copy-start | bytes 3993604
  105.8 10.5 %collective-permute-start.7 = (f32[2,8,32,1,130]{4,2,3,1,0:T(8,128)S(1)}, f32[2,8,32,1,130]{4,2,3,1,0:T(8,128)S(1)}, u32[]{:S(2)}, u32[]{:S(2)}) collective-permute-start(f32[2,8,32,1,130]{4,2,3,1,0:T(8,128)S(1)} %get-tuple-element.21), channel_id=1, source_target_pairs={{1,0},{2,1},{3,2},{4,3},{5,4},{6,5},{7,6},{9,8},{10,9},{11,10},{12... | collective-permute-start | bytes 798728 | tf_op jit(solution)/shard_map/ppermute | solution.py:20
  107.7 9.8 %collective-permute-start.6 = (f32[2,8,32,1,130]{4,2,3,1,0:T(8,128)S(1)}, f32[2,8,32,1,130]{4,2,3,1,0:T(8,128)S(1)}, u32[]{:S(2)}, u32[]{:S(2)}) collective-permute-start(f32[2,8,32,1,130]{4,2,3,1,0:T(8,128)S(1)} %get-tuple-element.20), channel_id=1, source_target_pairs={{0,1},{1,2},{2,3},{3,4},{4,5},{5,6},{6,7},{8,9},{9,10},{10,11},{11... | collective-permute-start | bytes 798728 | tf_op jit(solution)/shard_map/ppermute | solution.py:18
  113.1 4.4 %copy-start.1 = (f32[2,8,32,8,1]{4,2,3,1,0:T(8,128)S(1)}, f32[2,8,32,8,1]{4,2,3,1,0:T(8,128)}, u32[]{:S(2)}) copy-start(f32[2,8,32,8,1]{4,2,3,1,0:T(8,128)} %copy.240) | copy-start | bytes 49156
  113.1 4.4 %copy-start.9 = (f32[1,8,32,8,128]{4,2,3,1,0:T(8,128)S(1)}, f32[1,8,32,8,128]{4,2,3,1,0:T(8,128)}, u32[]{:S(2)}) copy-start(f32[1,8,32,8,128]{4,2,3,1,0:T(8,128)} %copy-done.8) | copy-start | bytes 3145732
  113.1 4.4 %copy-start.11 = (f32[1,8,32,8,128]{4,2,3,1,0:T(8,128)S(1)}, f32[1,8,32,8,128]{4,2,3,1,0:T(8,128)}, u32[]{:S(2)}) copy-start(f32[1,8,32,8,128]{4,2,3,1,0:T(8,128)} %copy-done.10) | copy-start | bytes 3145732
  122.6 9.2 %copy-start.13 = (f32[8,32,10,130]{3,1,2,0:T(8,128)}, f32[8,32,10,130]{3,1,2,0:T(8,128)S(1)}, u32[]{:S(2)}) copy-start(f32[8,32,10,130]{3,1,2,0:T(8,128)S(1)} %get-tuple-element.22) | copy-start | bytes 3993604
  122.6 9.2 %copy-start.14 = (f32[8,32,10,130]{3,1,2,0:T(8,128)}, f32[8,32,10,130]{3,1,2,0:T(8,128)S(1)}, u32[]{:S(2)}) copy-start(f32[8,32,10,130]{3,1,2,0:T(8,128)S(1)} %get-tuple-element.23) | copy-start | bytes 3993604
  122.6 9.2 %copy-start.15 = (f32[8,32,10,130]{3,1,2,0:T(8,128)}, f32[8,32,10,130]{3,1,2,0:T(8,128)S(1)}, u32[]{:S(2)}) copy-start(f32[8,32,10,130]{3,1,2,0:T(8,128)S(1)} %get-tuple-element.24) | copy-start | bytes 3993604
  135.2 7.6 %collective-permute-start.13 = (f32[8,32,8,1]{1,2,3,0:T(8,128)S(1)}, f32[8,32,8,1]{1,2,3,0:T(8,128)S(1)}, u32[]{:S(2)}, u32[]{:S(2)}) collective-permute-start(f32[8,32,8,1]{1,2,3,0:T(8,128)S(1)} %copy.251), channel_id=1, source_target_pairs={{8,0},{16,8},{24,16},{9,1},{17,9},{25,17},{10,2},{18,10},{26,18},{... | collective-permute-start | bytes 24584 | tf_op jit(solution)/shard_map/ppermute | solution.py:20
  140.9 5.6 %collective-permute-start.12 = (f32[8,32,8,1]{1,2,3,0:T(8,128)S(1)}, f32[8,32,8,1]{1,2,3,0:T(8,128)S(1)}, u32[]{:S(2)}, u32[]{:S(2)}) collective-permute-start(f32[8,32,8,1]{1,2,3,0:T(8,128)S(1)} %copy.250), channel_id=1, source_target_pairs={{0,8},{8,16},{16,24},{1,9},{9,17},{17,25},{2,10},{10,18},{18,26},{... | collective-permute-start | bytes 24584 | tf_op jit(solution)/shard_map/ppermute | solution.py:18
  147.9 12.6 %copy-start.20 = (f32[8,32,8,1]{3,1,2,0:T(8,128)S(1)}, f32[8,32,8,1]{3,1,2,0:T(8,128)}, u32[]{:S(2)}) copy-start(f32[8,32,8,1]{3,1,2,0:T(8,128)} %copy.253) | copy-start | bytes 24580
  147.9 12.6 %copy-start.22 = (f32[8,32,8,1]{3,1,2,0:T(8,128)S(1)}, f32[8,32,8,1]{3,1,2,0:T(8,128)}, u32[]{:S(2)}) copy-start(f32[8,32,8,1]{3,1,2,0:T(8,128)} %copy.252) | copy-start | bytes 24580
  149.4 9.9 %collective-permute-start.15 = (f32[8,32,1,130]{3,1,2,0:T(8,128)S(1)}, f32[8,32,1,130]{3,1,2,0:T(8,128)S(1)}, u32[]{:S(2)}, u32[]{:S(2)}) collective-permute-start(f32[8,32,1,130]{3,1,2,0:T(8,128)S(1)} %get-tuple-element.31), channel_id=1, source_target_pairs={{1,0},{2,1},{3,2},{4,3},{5,4},{6,5},{7,6},{9,8},{10,9},{11,10},{12... | collective-permute-start | bytes 399368 | tf_op jit(solution)/shard_map/ppermute | solution.py:20
  151.4 9.1 %collective-permute-start.14 = (f32[8,32,1,130]{3,1,2,0:T(8,128)S(1)}, f32[8,32,1,130]{3,1,2,0:T(8,128)S(1)}, u32[]{:S(2)}, u32[]{:S(2)}) collective-permute-start(f32[8,32,1,130]{3,1,2,0:T(8,128)S(1)} %get-tuple-element.30), channel_id=1, source_target_pairs={{0,1},{1,2},{2,3},{3,4},{4,5},{5,6},{6,7},{8,9},{9,10},{10,11},{11... | collective-permute-start | bytes 399368 | tf_op jit(solution)/shard_map/ppermute | solution.py:18
  175.4 7.0 %collective-permute-start.17 = (f32[8,32,8,1]{1,2,3,0:T(8,128)S(1)}, f32[8,32,8,1]{1,2,3,0:T(8,128)S(1)}, u32[]{:S(2)}, u32[]{:S(2)}) collective-permute-start(f32[8,32,8,1]{1,2,3,0:T(8,128)S(1)} %copy.256), channel_id=1, source_target_pairs={{8,0},{16,8},{24,16},{9,1},{17,9},{25,17},{10,2},{18,10},{26,18},{... | collective-permute-start | bytes 24584 | tf_op jit(solution)/shard_map/ppermute | solution.py:20
  179.0 5.6 %collective-permute-start.16 = (f32[8,32,8,1]{1,2,3,0:T(8,128)S(1)}, f32[8,32,8,1]{1,2,3,0:T(8,128)S(1)}, u32[]{:S(2)}, u32[]{:S(2)}) collective-permute-start(f32[8,32,8,1]{1,2,3,0:T(8,128)S(1)} %copy.255), channel_id=1, source_target_pairs={{0,8},{8,16},{16,24},{1,9},{9,17},{17,25},{2,10},{10,18},{18,26},{... | collective-permute-start | bytes 24584 | tf_op jit(solution)/shard_map/ppermute | solution.py:18
  186.0 12.3 %copy-start.21 = (f32[8,32,8,1]{3,1,2,0:T(8,128)S(1)}, f32[8,32,8,1]{3,1,2,0:T(8,128)}, u32[]{:S(2)}) copy-start(f32[8,32,8,1]{3,1,2,0:T(8,128)} %copy.258) | copy-start | bytes 24580
  186.0 12.3 %copy-start.23 = (f32[8,32,8,1]{3,1,2,0:T(8,128)S(1)}, f32[8,32,8,1]{3,1,2,0:T(8,128)}, u32[]{:S(2)}) copy-start(f32[8,32,8,1]{3,1,2,0:T(8,128)} %copy.257) | copy-start | bytes 24580
  187.5 9.6 %collective-permute-start.19 = (f32[8,32,1,130]{3,1,2,0:T(8,128)S(1)}, f32[8,32,1,130]{3,1,2,0:T(8,128)S(1)}, u32[]{:S(2)}, u32[]{:S(2)}) collective-permute-start(f32[8,32,1,130]{3,1,2,0:T(8,128)S(1)} %get-tuple-element.29), channel_id=1, source_target_pairs={{1,0},{2,1},{3,2},{4,3},{5,4},{6,5},{7,6},{9,8},{10,9},{11,10},{12... | collective-permute-start | bytes 399368 | tf_op jit(solution)/shard_map/ppermute | solution.py:20
  189.5 8.8 %collective-permute-start.18 = (f32[8,32,1,130]{3,1,2,0:T(8,128)S(1)}, f32[8,32,1,130]{3,1,2,0:T(8,128)S(1)}, u32[]{:S(2)}, u32[]{:S(2)}) collective-permute-start(f32[8,32,1,130]{3,1,2,0:T(8,128)S(1)} %get-tuple-element.28), channel_id=1, source_target_pairs={{0,1},{1,2},{2,3},{3,4},{4,5},{5,6},{6,7},{8,9},{9,10},{10,11},{11... | collective-permute-start | bytes 399368 | tf_op jit(solution)/shard_map/ppermute | solution.py:18
  203.2 21.0 %copy-start.30 = (f32[32,8,128]{2,1,0:T(8,128)S(1)}, f32[32,8,128]{2,1,0:T(8,128)}, u32[]{:S(2)}) copy-start(f32[32,8,128]{2,1,0:T(8,128)} %param.10) | copy-start | bytes 393220
  209.4 5.3 %collective-permute-start.20 = (f32[32,8,1]{0,1,2:T(8,128)S(1)}, f32[32,8,1]{0,1,2:T(8,128)S(1)}, u32[]{:S(2)}, u32[]{:S(2)}) collective-permute-start(f32[32,8,1]{0,1,2:T(8,128)S(1)} %get-tuple-element.50), channel_id=1, source_target_pairs={{8,0},{16,8},{24,16},{9,1},{17,9},{25,17},{10,2},{18,10},{26,18},{... | collective-permute-start | bytes 3080 | tf_op jit(solution)/shard_map/ppermute | solution.py:20
  211.3 5.3 %collective-permute-start.21 = (f32[32,8,1]{0,1,2:T(8,128)S(1)}, f32[32,8,1]{0,1,2:T(8,128)S(1)}, u32[]{:S(2)}, u32[]{:S(2)}) collective-permute-start(f32[32,8,1]{0,1,2:T(8,128)S(1)} %get-tuple-element.49), channel_id=1, source_target_pairs={{0,8},{8,16},{16,24},{1,9},{9,17},{17,25},{2,10},{10,18},{18,26},{... | collective-permute-start | bytes 3080 | tf_op jit(solution)/shard_map/ppermute | solution.py:18
  216.7 9.3 %collective-permute-start.23 = (f32[32,1,130]{0,1,2:T(1,128)S(1)}, f32[32,1,130]{0,1,2:T(1,128)S(1)}, u32[]{:S(2)}, u32[]{:S(2)}) collective-permute-start(f32[32,1,130]{0,1,2:T(1,128)S(1)} %get-tuple-element.48), channel_id=1, source_target_pairs={{0,1},{1,2},{2,3},{3,4},{4,5},{5,6},{6,7},{8,9},{9,10},{10,11},{11... | collective-permute-start | bytes 49928 | tf_op jit(solution)/shard_map/ppermute | solution.py:18
  222.2 5.6 %collective-permute-start.22 = (f32[32,1,130]{0,1,2:T(1,128)S(1)}, f32[32,1,130]{0,1,2:T(1,128)S(1)}, u32[]{:S(2)}, u32[]{:S(2)}) collective-permute-start(f32[32,1,130]{0,1,2:T(1,128)S(1)} %get-tuple-element.47), channel_id=1, source_target_pairs={{1,0},{2,1},{3,2},{4,3},{5,4},{6,5},{7,6},{9,8},{10,9},{11,10},{12... | collective-permute-start | bytes 49928 | tf_op jit(solution)/shard_map/ppermute | solution.py:20
  (10 other events, 24.8 us)
where the time goes:
time: 231 us; the launch traced here: 229 us
  starting transfers between devices  85.2 us (37%)
  other arithmetic  64.4 us (28%)
  local copies, waits for them, and re-layouts  63.9 us (28%)
  waiting for transfers between devices  14.2 us (6%)
    ppermute x12, starting transfers between devices, with_halo(): lax.ppermute(tail, axis, [(i, (i + 1) % count) for i in range(ends)])  44.8 us
    ppermute x12, starting transfers between devices, with_halo(): lax.ppermute(head, axis, [((i + 1) % count, i) for i in range(ends)])  28 us
    div x2, other arithmetic, relax(): return (source[:, :, 1:-1, 1:-1] + inflow) / denominator[:, :, 1:-1, 1:-1]  14.4 us
    slice x8, local copies, waits for them, and re-layouts, with_halo(): lax.slice_in_dim(cells, cells.shape[dim] - width, cells.shape[dim], axis=...  13.2 us
    unnamed x75, local copies, waits for them, and re-layouts  10.8 us
    reshape x1, local copies, waits for them, and re-layouts, shards(): source.at[:, target].add(rows_in.T, mode='drop')  10.6 us
    ppermute x5, local copies, waits for them, and re-layouts, with_halo(): lax.ppermute(tail, axis, [(i, (i + 1) % count) for i in range(ends)])  8.64 us
    slice x5, local copies, waits for them, and re-layouts, relax(): vertical = plus_z[:, :-2] + minus_z[:, 2:]  8.51 us
  transfers between devices with their start and end apart: 26, of which 9 were waited for; matrix products, arithmetic and copies ran while one was open for 29% of the time, Pallas kernels for 0%

commit v1 on v0

v1 whole, which is shorter than its diff:
```python
import functools

import jax
import jax.numpy as jnp
from jax import lax
from jax.experimental import pallas as pl
from jax.experimental.pallas import tpu as pltpu
from jax.sharding import PartitionSpec as P

SWEEPS = 3
CAP = 4
MESH = pl.DeviceIdType.MESH
F32 = jnp.float32
BF16 = jnp.bfloat16
FIELDS = 32


def roll(x, shift, axis):
    return pltpu.roll(x, shift % x.shape[axis], axis)


def kernel(
    n_gx, n_gy,
    t_h, a_h, f_h, slow_h, rows_h, tile_h, cell_h,
    adj_h, grad_h,
    tv, fv, a0, a1, slv, rowsv, tilev, cellv, gradv,
    c_l, c_r, c_u, c_d, c_b, c_t, sp, total,
    rec, msg, box,
    ey_hi, ey_lo, ex, ry_hi, ry_lo, rx,
    oy_hi, oy_lo, ox, iy_lo, iy_hi, ix_lo, ix_hi,
    toy_hi, toy_lo, tox, tiy_lo, tiy_hi, tix_lo, tix_hi,
    in_sem, small_sem, send_sem, recv_sem, tsend, trecv, st_send, st_recv, out_sem,
):
    sources, levels, rows_n, lanes_n = tv.shape
    devices = n_gx * n_gy
    mx = lax.axis_index("gx")
    my = lax.axis_index("gy")
    me = mx * n_gy + my

    barrier = pltpu.get_barrier_semaphore()
    others = [(dx, dy) for dx in range(n_gx) for dy in range(n_gy) if dx or dy]

    def far(dx, dy):
        return lax.rem(mx + dx, n_gx), lax.rem(my + dy, n_gy)

    for dx, dy in others:
        pl.semaphore_signal(barrier, inc=1, device_id=far(dx, dy), device_id_type=MESH)

    small = [
        pltpu.make_async_copy(src, dst, small_sem.at[k])
        for k, (src, dst) in enumerate(
            [(tile_h, tilev), (rows_h, rowsv), (cell_h, cellv), (slow_h, slv)]
        )
    ]
    for copy in small:
        copy.start()

    def load(k, src, dst, s):
        return pltpu.make_async_copy(src.at[s], dst.at[s], in_sem.at[k, s])

    for k, (src, dst) in enumerate([(t_h, tv), (a_h, a0), (f_h, fv)]):
        for s in range(sources):
            load(k, src, dst, s).start()

    sub = lax.broadcasted_iota(jnp.int32, (rows_n, lanes_n), 0)
    lane = lax.broadcasted_iota(jnp.int32, (rows_n, lanes_n), 1)
    first_row, last_row = sub == 0, sub == rows_n - 1
    first_lane, last_lane = lane == 0, lane == lanes_n - 1
    odd = lane % 2 == 1

    @pl.when(my == 0)
    def _():
        iy_lo[...] = jnp.zeros_like(iy_lo)
        tiy_lo[...] = jnp.zeros_like(tiy_lo)

    @pl.when(my == n_gy - 1)
    def _():
        iy_hi[...] = jnp.zeros_like(iy_hi)
        tiy_hi[...] = jnp.zeros_like(tiy_hi)

    @pl.when(mx == 0)
    def _():
        ix_lo[...] = jnp.zeros_like(ix_lo)
        tix_lo[...] = jnp.zeros_like(tix_lo)

    @pl.when(mx == n_gx - 1)
    def _():
        ix_hi[...] = jnp.zeros_like(ix_hi)
        tix_hi[...] = jnp.zeros_like(tix_hi)

    for copy in small[:3]:
        copy.wait()
    count = rowsv.shape[0]
    r_i = lax.broadcasted_iota(jnp.int32, (count, count), 0)
    c_i = lax.broadcasted_iota(jnp.int32, (count, count), 1)
    eye = r_i == c_i
    tile_row = jnp.sum(jnp.where(eye, tilev[...].astype(F32), 0.0), axis=0, keepdims=True)
    cell_col = jnp.sum(jnp.where(eye, cellv[...].astype(F32), 0.0), axis=1, keepdims=True)
    cell_row_f = jnp.floor(cell_col * (1.0 / lanes_n))
    rec[...] = jnp.zeros_like(rec)
    rec[:, 0:sources] = rowsv[...]
    rec[:, sources : sources + 1] = cell_row_f
    rec[:, sources + 1 : sources + 2] = cell_col - cell_row_f * lanes_n
    d_i = lax.broadcasted_iota(jnp.int32, (devices, count), 0).astype(F32)
    named = jnp.where(d_i == tile_row, 1.0, 0.0)
    earlier = jnp.where(r_i < c_i, 1.0, 0.0)
    rank = jnp.dot(named.astype(BF16), earlier.astype(BF16), preferred_element_type=F32)
    base = rec[...]
    b_hi = base.astype(BF16)
    left = base - b_hi.astype(F32)
    b_mid = left.astype(BF16)
    b_lo = (left - b_mid.astype(F32)).astype(BF16)
    slots = jnp.zeros((devices, lanes_n), F32)
    for c in range(CAP):
        pick = jnp.where((named > 0.0) & (rank == float(c)), 1.0, 0.0).astype(BF16)
        got = (
            jnp.dot(pick, b_lo, preferred_element_type=F32)
            + jnp.dot(pick, b_mid, preferred_element_type=F32)
            + jnp.dot(pick, b_hi, preferred_element_type=F32)
        )
        slots = slots + (roll(got, FIELDS * c, 1) if c else got)
    for d in range(devices):
        msg[d] = slots[d : d + 1, :]

    def packed(acc, plane, z):
        return jnp.where((lane == 2 * z) | (lane == 2 * z + 1), roll(plane, 2 * z + 1, 1), acc)

    def edges_of(s, _):
        load(0, t_h, tv, s).wait()
        load(1, a_h, a0, s).wait()
        acc_t = jnp.zeros((rows_n, lanes_n), F32)
        acc_a = jnp.zeros((rows_n, lanes_n), F32)
        for z in range(levels):
            t = tv[s, z]
            a = a0[s, z]
            oy_hi[0, s, z : z + 1, :] = t[rows_n - 1 : rows_n]
            oy_lo[0, s, z : z + 1, :] = t[0:1]
            ry_hi[s, z : z + 1, :] = a[rows_n - 1 : rows_n]
            ry_lo[s, z : z + 1, :] = a[0:1]
            acc_t = packed(acc_t, t, z)
            acc_a = packed(acc_a, a, z)
        ox[0, s] = acc_t
        rx[s] = acc_a
        return 0

    lax.fori_loop(0, sources, edges_of, 0)

    pl.semaphore_wait(barrier, devices - 1)

    def halo(k, s):
        def one(way, src, dst, dev):
            return pltpu.make_async_remote_copy(
                src_ref=src.at[k, s], dst_ref=dst.at[k, s],
                send_sem=send_sem.at[k, way, s], recv_sem=recv_sem.at[k, way, s],
                device_id=dev, device_id_type=MESH,
            )
        up = (mx, lax.rem(my + 1, n_gy))
        down = (mx, lax.rem(my + n_gy - 1, n_gy))
        right = (lax.rem(mx + 1, n_gx), my)
        left_ = (lax.rem(mx + n_gx - 1, n_gx), my)
        return (
            (one(0, oy_hi, iy_lo, up), my < n_gy - 1, my > 0),
            (one(1, oy_lo, iy_hi, down), my > 0, my < n_gy - 1),
            (one(2, ox, ix_lo, right), mx < n_gx - 1, mx > 0),
            (one(3, ox, ix_hi, left_), mx > 0, mx < n_gx - 1),
        )

    def send(k, s):
        for copy, sends, _ in halo(k, s):
            @pl.when(sends)
            def _(copy=copy):
                copy.start()

    def arrive(k, s):
        for copy, _, takes in halo(k, s):
            @pl.when(takes)
            def _(copy=copy):
                copy.wait_recv()

    def send_all(s, _):
        send(0, s)
        return 0

    lax.fori_loop(0, sources, send_all, 0)

    own = pltpu.make_async_copy(msg.at[me], box.at[me], st_recv)
    for dx, dy in others:
        ox_, oy_ = far(dx, dy)
        pltpu.make_async_remote_copy(
            src_ref=msg.at[ox_ * n_gy + oy_], dst_ref=box.at[me],
            send_sem=st_send, recv_sem=st_recv,
            device_id=(ox_, oy_), device_id_type=MESH,
        ).start()
    own.start()

    def coefficients(s, _):
        load(2, f_h, fv, s).wait()
        arrive(0, s)
        acc = jnp.zeros((rows_n, lanes_n), F32)
        comb = jnp.where(odd, ix_hi[0, s], ix_lo[0, s])
        below = jnp.zeros((rows_n, lanes_n), F32)
        z_plus_before = jnp.zeros((rows_n, lanes_n), F32)
        r_before = None
        t = tv[s, 0]
        for z in range(levels):
            above = tv[s, z + 1] if z + 1 < levels else jnp.zeros((rows_n, lanes_n), F32)
            flags = fv[s, z]
            is_x, is_y, is_z = (flags & 1) == 1, (flags & 2) == 2, (flags & 4) == 4
            u = roll(comb, -(2 * z + 1), 1)
            t_l = roll(jnp.where(last_lane, u, t), 1, 1)
            t_r = roll(jnp.where(first_lane, u, t), -1, 1)
            t_u = jnp.where(first_row, iy_lo[0, s, z : z + 1, :], roll(t, 1, 0))
            t_d = jnp.where(last_row, iy_hi[0, s, z : z + 1, :], roll(t, -1, 0))
            k_x = jnp.maximum(t - jnp.where(is_x, t_r, t_l), 0.0)
            k_y = jnp.maximum(t - jnp.where(is_y, t_d, t_u), 0.0)
            k_z = jnp.maximum(t - jnp.where(is_z, above, below), 0.0)
            r = 1.0 / (1.0 + k_x + k_y + k_z)
            x_plus, x_minus = jnp.where(is_x, k_x, 0.0), jnp.where(is_x, 0.0, k_x)
            y_plus, y_minus = jnp.where(is_y, k_y, 0.0), jnp.where(is_y, 0.0, k_y)
            z_plus, z_minus = jnp.where(is_z, k_z, 0.0), jnp.where(is_z, 0.0, k_z)
            c_l[s, z] = roll(jnp.where(last_lane, 1.0, x_plus), 1, 1) * r
            c_r[s, z] = roll(jnp.where(first_lane, 1.0, x_minus), -1, 1) * r
            c_u[s, z] = roll(jnp.where(last_row, 1.0, y_plus), 1, 0) * r
            c_d[s, z] = roll(jnp.where(first_row, 1.0, y_minus), -1, 0) * r
            c_b[s, z] = z_plus_before * r
            if z:
                c_t[s, z - 1] = z_minus * r_before
            sp[s, z] = r
            ey_hi[s, z : z + 1, :] = y_plus[rows_n - 1 : rows_n]
            ey_lo[s, z : z + 1, :] = y_minus[0:1]
            acc = packed(acc, jnp.where(first_lane, x_minus, x_plus), z)
            below, t = t, above
            z_plus_before, r_before = z_plus, r
        c_t[s, levels - 1] = jnp.zeros((rows_n, lanes_n), F32)
        ex[s] = acc
        oy_hi[1, s] = ey_hi[s] * ry_hi[s]
        oy_lo[1, s] = ey_lo[s] * ry_lo[s]
        ox[1, s] = acc * rx[s]
        send(1, s)
        return 0

    lax.fori_loop(0, sources, coefficients, 0)

    pltpu.make_async_copy(box, box, st_recv).wait()
    boxes = jnp.concatenate([box[d] for d in range(devices)], axis=0)
    stacked = jnp.concatenate(
        [boxes] + [roll(boxes, -FIELDS * c, 1) for c in range(1, CAP)], axis=0
    )
    fields = stacked.T
    amount = stacked.shape[0]
    values = fields[0:sources]
    v_hi = values.astype(BF16).astype(F32)
    v_left = values - v_hi
    v_mid = v_left.astype(BF16).astype(F32)
    v_lo = v_left - v_mid
    at_row = fields[sources : sources + 1]
    at_lane = fields[sources + 1 : sources + 2]
    row_i = lax.broadcasted_iota(jnp.int32, (levels * rows_n, amount), 0).astype(F32)
    lane_i = lax.broadcasted_iota(jnp.int32, (lanes_n, amount), 0).astype(F32)
    in_row = jnp.where(row_i == at_row, 1.0, 0.0).astype(BF16)
    in_lane = lane_i == at_lane
    for s in range(sources):
        spread = None
        for part in (v_lo, v_mid, v_hi):
            weights = jnp.where(in_lane, part[s : s + 1], 0.0).astype(BF16)
            term = lax.dot_general(
                in_row, weights, (((1,), (1,)), ((), ())), preferred_element_type=F32
            )
            spread = term if spread is None else spread + term
        sp[s] = sp[s] * spread.reshape(levels, rows_n, lanes_n)

    total[...] = jnp.zeros_like(total)

    def sweep(k, src, dst, s):
        last = k == SWEEPS
        arrive(k, s)
        acc = jnp.zeros((rows_n, lanes_n), F32)
        comb = jnp.where(odd, ix_hi[k, s], ix_lo[k, s])
        below = None
        a = src[s, 0]
        for z in range(levels):
            above = src[s, z + 1] if z + 1 < levels else None
            u = roll(comb, -(2 * z + 1), 1)
            a_l = roll(jnp.where(last_lane, u, a), 1, 1)
            a_r = roll(jnp.where(first_lane, u, a), -1, 1)
            a_u = jnp.where(first_row, iy_lo[k, s, z : z + 1, :], roll(a, 1, 0))
            a_d = jnp.where(last_row, iy_hi[k, s, z : z + 1, :], roll(a, -1, 0))
            out = (sp[s, z] + c_l[s, z] * a_l) + (c_r[s, z] * a_r + c_u[s, z] * a_u)
            out = out + c_d[s, z] * a_d
            if below is not None:
                out = out + c_b[s, z] * below
            if above is not None:
                out = out + c_t[s, z] * above
            dst[s, z] = out
            if last:
                total[z] = total[z] + out
            else:
                ry_hi[s, z : z + 1, :] = out[rows_n - 1 : rows_n]
                ry_lo[s, z : z + 1, :] = out[0:1]
                acc = packed(acc, out, z)
            below, a = a, above
        if last:
            pltpu.make_async_copy(dst.at[s], adj_h.at[s], out_sem.at[s]).start()
        else:
            oy_hi[k + 1, s] = ey_hi[s] * ry_hi[s]
            oy_lo[k + 1, s] = ey_lo[s] * ry_lo[s]
            ox[k + 1, s] = ex[s] * acc
            send(k + 1, s)
        return 0

    held = (a0, a1)
    for k in range(1, SWEEPS + 1):
        src, dst = held[(k - 1) % 2], held[k % 2]
        lax.fori_loop(0, sources, lambda s, _, k=k, src=src, dst=dst: sweep(k, src, dst, s), 0)
    result = held[SWEEPS % 2]

    acc = jnp.zeros((rows_n, lanes_n), F32)
    for z in range(levels):
        cells = total[z]
        toy_hi[z : z + 1, :] = cells[rows_n - 1 : rows_n]
        toy_lo[z : z + 1, :] = cells[0:1]
        acc = packed(acc, cells, z)
    tox[...] = acc

    def last_copy(way, src, dst, dev):
        return pltpu.make_async_remote_copy(
            src_ref=src, dst_ref=dst, send_sem=tsend.at[way], recv_sem=trecv.at[way],
            device_id=dev, device_id_type=MESH,
        )

    finals = (
        (last_copy(0, toy_hi, tiy_lo, (mx, lax.rem(my + 1, n_gy))), my < n_gy - 1, my > 0),
        (last_copy(1, toy_lo, tiy_hi, (mx, lax.rem(my + n_gy - 1, n_gy))), my > 0, my < n_gy - 1),
        (last_copy(2, tox, tix_lo, (lax.rem(mx + 1, n_gx), my)), mx < n_gx - 1, mx > 0),
        (last_copy(3, tox, tix_hi, (lax.rem(mx + n_gx - 1, n_gx), my)), mx > 0, mx < n_gx - 1),
    )
    for copy, sends, _ in finals:
        @pl.when(sends)
        def _(copy=copy):
            copy.start()

    def drained(s, _):
        for k in range(SWEEPS + 1):
            for copy, sends, _ in halo(k, s):
                @pl.when(sends)
                def _(copy=copy):
                    copy.wait_send()
        return 0

    lax.fori_loop(0, sources, drained, 0)
    rest = msg.at[pl.ds(0, devices - 1)]
    pltpu.make_async_copy(rest, rest, st_send).wait()
    small[3].wait()

    for copy, _, takes in finals:
        @pl.when(takes)
        def _(copy=copy):
            copy.wait_recv()

    comb = jnp.where(odd, tix_hi[...], tix_lo[...])
    for z in range(levels):
        cells = total[z]
        u = roll(comb, -(2 * z + 1), 1)
        beside = (
            roll(jnp.where(last_lane, u, cells), 1, 1)
            + roll(jnp.where(first_lane, u, cells), -1, 1)
        ) + (
            jnp.where(first_row, tiy_lo[z : z + 1, :], roll(cells, 1, 0))
            + jnp.where(last_row, tiy_hi[z : z + 1, :], roll(cells, -1, 0))
        )
        gradv[z] = slv[z] * (cells + 0.125 * (beside - 4.0 * cells))
    out_grad = pltpu.make_async_copy(gradv, grad_h, out_sem.at[sources])
    out_grad.start()
    for copy, sends, _ in finals:
        @pl.when(sends)
        def _(copy=copy):
            copy.wait_send()
    for s in range(sources):
        pltpu.make_async_copy(result.at[s], adj_h.at[s], out_sem.at[s]).wait()
    out_grad.wait()


def shards(
    n_gx, n_gy,
    traveltime, adjoint_start, upwind_flags, slowness, residual_rows, station_tile, station_cell,
):
    sources, levels, rows_n, lanes_n = traveltime.shape
    devices = n_gx * n_gy
    rounds = SWEEPS + 1
    big = pltpu.VMEM(traveltime.shape, F32)
    flat = pltpu.VMEM(slowness.shape, F32)
    yrows = pltpu.VMEM((sources, levels, lanes_n), F32)
    xcols = pltpu.VMEM((sources, rows_n, lanes_n), F32)
    ymsg = pltpu.VMEM((rounds, sources, levels, lanes_n), F32)
    xmsg = pltpu.VMEM((rounds, sources, rows_n, lanes_n), F32)
    ytot = pltpu.VMEM((levels, lanes_n), F32)
    xtot = pltpu.VMEM((rows_n, lanes_n), F32)
    count = residual_rows.shape[0]
    dma = pltpu.SemaphoreType.DMA
    return pl.pallas_call(
        functools.partial(kernel, n_gx, n_gy),
        out_shape=(
            jax.ShapeDtypeStruct(traveltime.shape, F32),
            jax.ShapeDtypeStruct(slowness.shape, F32),
        ),
        in_specs=[pl.BlockSpec(memory_space=pl.ANY)] * 7,
        out_specs=[pl.BlockSpec(memory_space=pl.ANY)] * 2,
        scratch_shapes=[
            big, pltpu.VMEM(traveltime.shape, jnp.int32), big, big, flat,
            pltpu.VMEM(residual_rows.shape, F32),
            pltpu.VMEM(station_tile.shape, jnp.int32),
            pltpu.VMEM((1, count), jnp.int32),
            flat,
            big, big, big, big, big, big, big, flat,
            pltpu.VMEM((count, lanes_n), F32),
            pltpu.VMEM((devices, 1, lanes_n), F32),
            pltpu.VMEM((devices, 1, lanes_n), F32),
            yrows, yrows, xcols, yrows, yrows, xcols,
            ymsg, ymsg, xmsg, ymsg, ymsg, xmsg, xmsg,
            ytot, ytot, xtot, ytot, ytot, xtot, xtot,
            dma((3, sources)), dma((4,)),
            dma((rounds, 4, sources)), dma((rounds, 4, sources)),
            dma((4,)), dma((4,)), dma, dma, dma((sources + 1,)),
        ],
        compiler_params=pltpu.CompilerParams(
            collective_id=0, has_side_effects=True, vmem_limit_bytes=32 * 1024 * 1024
        ),
        name="tomography",
    )(
        traveltime, adjoint_start, upwind_flags, slowness, residual_rows, station_tile,
        station_cell.reshape(1, count),
    )


def solution(mesh):
    wide = P(None, None, "gy", "gx")
    placed = (
        wide, wide, wide, P(None, "gy", "gx"),
        P(("gx", "gy"), None), P(("gx", "gy"), None), P(("gx", "gy")),
    )
    return jax.shard_map(
        functools.partial(shards, mesh.shape["gx"], mesh.shape["gy"]),
        mesh=mesh,
        in_specs=placed,
        out_specs=(wide, P(None, "gy", "gx")),
        check_vma=False,
    )
```

time: 231 us -> 41.5 us (0.18)
  the two profiles are of different devices: /device:TPU:5 before, /device:TPU:0 now
where the time goes in v1:
time: 41.5 us; the launch traced here: 41.3 us
  Pallas kernels  33 us (80%)
  local copies, waits for them, and re-layouts  7.63 us (18%)
  between operations  0.66 us (2%)
    pallas_call x1, Pallas kernels, shards(): pl.pallas_call(functools.partial(kernel, n_gx, n_gy), out_shape=(jax.Shap...  33 us
    unnamed x16, local copies, waits for them, and re-layouts  7.63 us

profile of v1, /device:TPU:0, one launch (start us, length us, event | category | flops | bytes accessed | tf_op | source)
XLA Modules:
  0.0 41.3 jit_solution(2196617129557069902)
XLA Ops:
  0.6 0.0 copy-start.5
  0.6 0.8 %copy.9.rows_h = f32[64,8]{1,0:T(8,128)S(1)} copy(f32[64,8]{0,1:T(8,128)} %param.11) | data formatting | bytes 4096 | tf_op args[4]
  1.4 0.0 copy-done.5
  1.4 0.0 copy-start.4
  1.4 0.1 copy.10.tile_h
  1.5 0.6 %copy-done.4 = s32[64]{0:T(128)S(1)} copy-done((s32[64]{0:T(128)S(1)}, s32[64]{0:T(128)}, u32[]{:S(2)}) %copy-start.4) | copy-done | bytes 280
  2.1 0.0 copy-start
  2.1 1.2 %copy-done = f32[8,32,8,128]{3,2,1,0:T(8,128)S(1)} copy-done((f32[8,32,8,128]{3,2,1,0:T(8,128)S(1)}, f32[8,32,8,128]{3,2,1,0:T(8,128)}, u32[]{:S(2)}) %copy-start) | copy-done | bytes 1048600
  3.3 0.0 copy-start.1
  3.3 1.2 %copy-done.1 = f32[8,32,8,128]{3,2,1,0:T(8,128)S(1)} copy-done((f32[8,32,8,128]{3,2,1,0:T(8,128)S(1)}, f32[8,32,8,128]{3,2,1,0:T(8,128)}, u32[]{:S(2)}) %copy-start.1) | copy-done | bytes 1048600
  4.5 0.0 copy-start.2
  4.5 1.2 %copy-done.2 = s32[8,32,8,128]{3,2,1,0:T(8,128)S(1)} copy-done((s32[8,32,8,128]{3,2,1,0:T(8,128)S(1)}, s32[8,32,8,128]{3,2,1,0:T(8,128)}, u32[]{:S(2)}) %copy-start.2) | copy-done | bytes 1048600
  5.8 0.0 copy-start.3
  5.8 0.9 %copy-done.3 = f32[32,8,128]{2,1,0:T(8,128)S(1)} copy-done((f32[32,8,128]{2,1,0:T(8,128)S(1)}, f32[32,8,128]{2,1,0:T(8,128)}, u32[]{:S(2)}) %copy-start.3) | copy-done | bytes 131096
  6.7 33.0 %tomography.1 = (f32[8,32,8,128]{3,2,1,0:T(8,128)S(1)}, f32[32,8,128]{2,1,0:T(8,128)S(1)}) custom-call(f32[8,32,8,128]{3,2,1,0:T(8,128)S(1)} %copy-done, f32[8,32,8,128]{3,2,1,0:T(8,128)S(1)} %copy-done.1, s32[8,32,8,128]{3,2,1,0:T(8,128)S(1)} %copy-done.2, f32[32,8,128]{2,1,0:T(8,128)S(1)} %copy-done.3, f32[64,8]{1,0:T(8,128)S(1)} %copy.9.rows_h, ...), custom_call_target="tpu_custom_call" | custom-call | tf_op jit(solution)/shard_map/tomography/pallas_call | solution.py:400
  39.6 1.0 %copy.13 = f32[8,32,8,128]{3,2,1,0:T(8,128)} copy(f32[8,32,8,128]{3,2,1,0:T(8,128)S(1)} %get-tuple-element.4) | data formatting | bytes 2097152
  40.6 0.7 %copy.14 = f32[32,8,128]{2,1,0:T(8,128)} copy(f32[32,8,128]{2,1,0:T(8,128)S(1)} %get-tuple-element.5) | data formatting | bytes 262144
Async XLA Ops:
  0.6 0.8 %copy-start.5 = (s32[64,1]{0,1:T(1,128)S(1)}, s32[64,1]{0,1:T(1,128)}, u32[]{:S(2)}) copy-start(s32[64,1]{0,1:T(1,128)} %param.12) | copy-start | bytes 772
  1.4 0.7 %copy-start.4 = (s32[64]{0:T(128)S(1)}, s32[64]{0:T(128)}, u32[]{:S(2)}) copy-start(s32[64]{0:T(128)} %param.13) | copy-start | bytes 772
  2.1 1.2 %copy-start = (f32[8,32,8,128]{3,2,1,0:T(8,128)S(1)}, f32[8,32,8,128]{3,2,1,0:T(8,128)}, u32[]{:S(2)}) copy-start(f32[8,32,8,128]{3,2,1,0:T(8,128)} %t_h.1) | copy-start | bytes 3145732
  3.3 1.2 %copy-start.1 = (f32[8,32,8,128]{3,2,1,0:T(8,128)S(1)}, f32[8,32,8,128]{3,2,1,0:T(8,128)}, u32[]{:S(2)}) copy-start(f32[8,32,8,128]{3,2,1,0:T(8,128)} %a_h.1) | copy-start | bytes 3145732
  4.5 1.2 %copy-start.2 = (s32[8,32,8,128]{3,2,1,0:T(8,128)S(1)}, s32[8,32,8,128]{3,2,1,0:T(8,128)}, u32[]{:S(2)}) copy-start(s32[8,32,8,128]{3,2,1,0:T(8,128)} %f_h.1) | copy-start | bytes 3145732
  5.8 0.9 %copy-start.3 = (f32[32,8,128]{2,1,0:T(8,128)S(1)}, f32[32,8,128]{2,1,0:T(8,128)}, u32[]{:S(2)}) copy-start(f32[32,8,128]{2,1,0:T(8,128)} %slow_h.1) | copy-start | bytes 393220

commit v2 on v1

--- a/solution.py
+++ b/solution.py
@@ -19,17 +19,21 @@
     return pltpu.roll(x, shift % x.shape[axis], axis)
 
 
+def across(a, b):
+    return lax.dot_general(a, b, (((1,), (1,)), ((), ())), preferred_element_type=F32)
+
+
 def kernel(
     n_gx, n_gy,
     t_h, a_h, f_h, slow_h, rows_h, tile_h, cell_h,
-    adj_h, grad_h,
-    tv, fv, a0, a1, slv, rowsv, tilev, cellv, gradv,
+    adjv, gradv,
+    tv, fv, a0, slv, rowsv, tilev, cellv,
     c_l, c_r, c_u, c_d, c_b, c_t, sp, total,
     rec, msg, box,
     ey_hi, ey_lo, ex, ry_hi, ry_lo, rx,
     oy_hi, oy_lo, ox, iy_lo, iy_hi, ix_lo, ix_hi,
     toy_hi, toy_lo, tox, tiy_lo, tiy_hi, tix_lo, tix_hi,
-    in_sem, small_sem, send_sem, recv_sem, tsend, trecv, st_send, st_recv, out_sem,
+    in_sem, small_sem, send_sem, recv_sem, tsend, trecv, st_send, st_recv,
 ):
     sources, levels, rows_n, lanes_n = tv.shape
     devices = n_gx * n_gy
@@ -90,18 +94,16 @@
 
     for copy in small[:3]:
         copy.wait()
-    count = rowsv.shape[0]
+    count = rowsv.shape[1]
     r_i = lax.broadcasted_iota(jnp.int32, (count, count), 0)
     c_i = lax.broadcasted_iota(jnp.int32, (count, count), 1)
-    eye = r_i == c_i
-    tile_row = jnp.sum(jnp.where(eye, tilev[...].astype(F32), 0.0), axis=0, keepdims=True)
-    cell_col = jnp.sum(jnp.where(eye, cellv[...].astype(F32), 0.0), axis=1, keepdims=True)
-    cell_row_f = jnp.floor(cell_col * (1.0 / lanes_n))
+    tile_row = tilev[...]
+    cells = cellv[...]
     rec[...] = jnp.zeros_like(rec)
-    rec[:, 0:sources] = rowsv[...]
-    rec[:, sources : sources + 1] = cell_row_f
-    rec[:, sources + 1 : sources + 2] = cell_col - cell_row_f * lanes_n
-    d_i = lax.broadcasted_iota(jnp.int32, (devices, count), 0).astype(F32)
+    rec[0:sources] = rowsv[...]
+    rec[sources : sources + 1] = (cells // lanes_n).astype(F32)
+    rec[sources + 1 : sources + 2] = (cells % lanes_n).astype(F32)
+    d_i = lax.broadcasted_iota(jnp.int32, (devices, count), 0)
     named = jnp.where(d_i == tile_row, 1.0, 0.0)
     earlier = jnp.where(r_i < c_i, 1.0, 0.0)
     rank = jnp.dot(named.astype(BF16), earlier.astype(BF16), preferred_element_type=F32)
@@ -114,9 +116,7 @@
     for c in range(CAP):
         pick = jnp.where((named > 0.0) & (rank == float(c)), 1.0, 0.0).astype(BF16)
         got = (
-            jnp.dot(pick, b_lo, preferred_element_type=F32)
-            + jnp.dot(pick, b_mid, preferred_element_type=F32)
-            + jnp.dot(pick, b_hi, preferred_element_type=F32)
+            across(pick, b_lo) + across(pick, b_mid) + across(pick, b_hi)
         )
         slots = slots + (roll(got, FIELDS * c, 1) if c else got)
     for d in range(devices):
@@ -263,9 +263,7 @@
         spread = None
         for part in (v_lo, v_mid, v_hi):
             weights = jnp.where(in_lane, part[s : s + 1], 0.0).astype(BF16)
-            term = lax.dot_general(
-                in_row, weights, (((1,), (1,)), ((), ())), preferred_element_type=F32
-            )
+            term = across(in_row, weights)
             spread = term if spread is None else spread + term
         sp[s] = sp[s] * spread.reshape(levels, rows_n, lanes_n)
 
@@ -299,20 +297,17 @@
                 ry_lo[s, z : z + 1, :] = out[0:1]
                 acc = packed(acc, out, z)
             below, a = a, above
-        if last:
-            pltpu.make_async_copy(dst.at[s], adj_h.at[s], out_sem.at[s]).start()
-        else:
+        if not last:
             oy_hi[k + 1, s] = ey_hi[s] * ry_hi[s]
             oy_lo[k + 1, s] = ey_lo[s] * ry_lo[s]
             ox[k + 1, s] = ex[s] * acc
             send(k + 1, s)
         return 0
 
-    held = (a0, a1)
+    held = (a0, adjv)
     for k in range(1, SWEEPS + 1):
         src, dst = held[(k - 1) % 2], held[k % 2]
         lax.fori_loop(0, sources, lambda s, _, k=k, src=src, dst=dst: sweep(k, src, dst, s), 0)
-    result = held[SWEEPS % 2]
 
     acc = jnp.zeros((rows_n, lanes_n), F32)
     for z in range(levels):
@@ -369,15 +364,21 @@
             + jnp.where(last_row, tiy_hi[z : z + 1, :], roll(cells, -1, 0))
         )
         gradv[z] = slv[z] * (cells + 0.125 * (beside - 4.0 * cells))
-    out_grad = pltpu.make_async_copy(gradv, grad_h, out_sem.at[sources])
-    out_grad.start()
     for copy, sends, _ in finals:
         @pl.when(sends)
         def _(copy=copy):
             copy.wait_send()
-    for s in range(sources):
-        pltpu.make_async_copy(result.at[s], adj_h.at[s], out_sem.at[s]).wait()
-    out_grad.wait()
+
+
+def deliver(adj_v, grad_v, adj_h, grad_h, sem):
+    copies = [
+        pltpu.make_async_copy(adj_v, adj_h, sem.at[0]),
+        pltpu.make_async_copy(grad_v, grad_h, sem.at[1]),
+    ]
+    for copy in copies:
+        copy.start()
+    for copy in copies:
+        copy.wait()
 
 
 def shards(
@@ -397,22 +398,25 @@
     xtot = pltpu.VMEM((rows_n, lanes_n), F32)
     count = residual_rows.shape[0]
     dma = pltpu.SemaphoreType.DMA
-    return pl.pallas_call(
+    operands = (
+        traveltime, adjoint_start, upwind_flags, slowness, residual_rows.T,
+        station_tile.reshape(1, count), station_cell.reshape(1, count),
+    )
+    results = pl.pallas_call(
         functools.partial(kernel, n_gx, n_gy),
         out_shape=(
             jax.ShapeDtypeStruct(traveltime.shape, F32),
             jax.ShapeDtypeStruct(slowness.shape, F32),
         ),
-        in_specs=[pl.BlockSpec(memory_space=pl.ANY)] * 7,
-        out_specs=[pl.BlockSpec(memory_space=pl.ANY)] * 2,
+        in_specs=[pl.BlockSpec(memory_space=pltpu.HBM)] * 7,
+        out_specs=[pl.BlockSpec(memory_space=pltpu.VMEM)] * 2,
         scratch_shapes=[
-            big, pltpu.VMEM(traveltime.shape, jnp.int32), big, big, flat,
-            pltpu.VMEM(residual_rows.shape, F32),
-            pltpu.VMEM(station_tile.shape, jnp.int32),
+            big, pltpu.VMEM(traveltime.shape, jnp.int32), big, flat,
+            pltpu.VMEM((sources, count), F32),
             pltpu.VMEM((1, count), jnp.int32),
-            flat,
+            pltpu.VMEM((1, count), jnp.int32),
             big, big, big, big, big, big, big, flat,
-            pltpu.VMEM((count, lanes_n), F32),
+            pltpu.VMEM((lanes_n, count), F32),
             pltpu.VMEM((devices, 1, lanes_n), F32),
             pltpu.VMEM((devices, 1, lanes_n), F32),
             yrows, yrows, xcols, yrows, yrows, xcols,
@@ -420,16 +424,25 @@
             ytot, ytot, xtot, ytot, ytot, xtot, xtot,
             dma((3, sources)), dma((4,)),
             dma((rounds, 4, sources)), dma((rounds, 4, sources)),
-            dma((4,)), dma((4,)), dma, dma, dma((sources + 1,)),
+            dma((4,)), dma((4,)), dma, dma,
         ],
         compiler_params=pltpu.CompilerParams(
             collective_id=0, has_side_effects=True, vmem_limit_bytes=32 * 1024 * 1024
         ),
         name="tomography",
-    )(
-        traveltime, adjoint_start, upwind_flags, slowness, residual_rows, station_tile,
-        station_cell.reshape(1, count),
-    )
+    )(*[pltpu.with_memory_space_constraint(v, pltpu.HBM) for v in operands])
+    return pl.pallas_call(
+        deliver,
+        out_shape=(
+            jax.ShapeDtypeStruct(traveltime.shape, F32),
+            jax.ShapeDtypeStruct(slowness.shape, F32),
+        ),
+        in_specs=[pl.BlockSpec(memory_space=pltpu.VMEM)] * 2,
+        out_specs=[pl.BlockSpec(memory_space=pltpu.HBM)] * 2,
+        scratch_shapes=[dma((2,))],
+        compiler_params=pltpu.CompilerParams(vmem_limit_bytes=4 * 1024 * 1024),
+        name="deliver",
+    )(*results)
 
 
 def solution(mesh):

time: 41.5 us -> 30.5 us (0.73)
  local copies, waits for them, and re-layouts: 7.63 us -> 0 us
  Pallas kernels: 33 us -> 29.8 us
    unnamed x16 -> x0, local copies, waits for them, and re-layouts: 7.63 us -> none
    pallas_call x1, Pallas kernels: 33 us -> 28.7 us  [shards(): pl.pallas_call(functools.partial(kernel, n_gx, n_gy), out_shape=(jax.Shap...]
    pallas_call x0 -> x1, Pallas kernels: none -> 1.02 us  [shards(): pl.pallas_call(deliver, out_shape=(jax.ShapeDtypeStruct(traveltime.shape,...]
where the time goes in v2:
time: 30.5 us; the launch traced here: 30.4 us
  Pallas kernels  29.8 us (98%)
  between operations  0.64 us (2%)
    pallas_call x1, Pallas kernels, shards(): pl.pallas_call(functools.partial(kernel, n_gx, n_gy), out_shape=(jax.Shap...  28.7 us
    pallas_call x1, Pallas kernels, shards(): pl.pallas_call(deliver, out_shape=(jax.ShapeDtypeStruct(traveltime.shape,...  1.02 us

profile of v2, /device:TPU:0, one launch (start us, length us, event | category | flops | bytes accessed | tf_op | source)
XLA Modules:
  0.0 30.4 jit_solution(10246798989206394503)
XLA Ops:
  0.6 28.7 %tomography.1 = (f32[8,32,8,128]{3,2,1,0:T(8,128)S(1)}, f32[32,8,128]{2,1,0:T(8,128)S(1)}) custom-call(f32[8,32,8,128]{3,2,1,0:T(8,128)} %t_h.1, f32[8,32,8,128]{3,2,1,0:T(8,128)} %a_h.1, s32[8,32,8,128]{3,2,1,0:T(8,128)} %f_h.1, f32[32,8,128]{2,1,0:T(8,128)} %slow_h.1, f32[8,64]{1,0:T(8,128)} %bitcast.3, s32[1,64]{1,0:T(1,128)} %bitcast.4, s32[1,64]{1,0:T(1,128)} %bitcast.5), custom_call_target="tpu_custom_call" | custom-call | tf_op jit(solution)/shard_map/tomography/pallas_call | solution.py:405
  29.4 1.0 %deliver.1 = (f32[8,32,8,128]{3,2,1,0:T(8,128)}, f32[32,8,128]{2,1,0:T(8,128)}) custom-call(f32[8,32,8,128]{3,2,1,0:T(8,128)S(1)} %get-tuple-element.4.adj_v, f32[32,8,128]{2,1,0:T(8,128)S(1)} %get-tuple-element.5.grad_v), custom_call_target="tpu_custom_call" | custom-call | tf_op jit(solution)/shard_map/deliver/pallas_call | solution.py:434

commit v3 on v2

--- a/solution.py
+++ b/solution.py
@@ -26,9 +26,9 @@
 def kernel(
     n_gx, n_gy,
     t_h, a_h, f_h, slow_h, rows_h, tile_h, cell_h,
-    adjv, gradv,
-    tv, fv, a0, slv, rowsv, tilev, cellv,
-    c_l, c_r, c_u, c_d, c_b, c_t, sp, total,
+    adjv, total, rows_lo, rows_hi, columns, slv,
+    tv, fv, a0, rowsv, tilev, cellv,
+    c_l, c_r, c_u, c_d, c_b, c_t, sp,
     rec, msg, box,
     ey_hi, ey_lo, ex, ry_hi, ry_lo, rx,
     oy_hi, oy_lo, ox, iy_lo, iy_hi, ix_lo, ix_hi,
@@ -53,9 +53,10 @@
     small = [
         pltpu.make_async_copy(src, dst, small_sem.at[k])
         for k, (src, dst) in enumerate(
-            [(tile_h, tilev), (rows_h, rowsv), (cell_h, cellv), (slow_h, slv)]
+            [(tile_h, tilev), (rows_h, rowsv), (cell_h, cellv)]
         )
     ]
+    slow = pltpu.make_async_copy(slow_h, slv, small_sem.at[3])
     for copy in small:
         copy.start()
 
@@ -65,12 +66,14 @@
     for k, (src, dst) in enumerate([(t_h, tv), (a_h, a0), (f_h, fv)]):
         for s in range(sources):
             load(k, src, dst, s).start()
+    slow.start()
 
     sub = lax.broadcasted_iota(jnp.int32, (rows_n, lanes_n), 0)
     lane = lax.broadcasted_iota(jnp.int32, (rows_n, lanes_n), 1)
     first_row, last_row = sub == 0, sub == rows_n - 1
     first_lane, last_lane = lane == 0, lane == lanes_n - 1
     odd = lane % 2 == 1
+    lane_pair = lane // 2
 
     @pl.when(my == 0)
     def _():
@@ -92,7 +95,7 @@
         ix_hi[...] = jnp.zeros_like(ix_hi)
         tix_hi[...] = jnp.zeros_like(tix_hi)
 
-    for copy in small[:3]:
+    for copy in small:
         copy.wait()
     count = rowsv.shape[1]
     r_i = lax.broadcasted_iota(jnp.int32, (count, count), 0)
@@ -123,7 +126,7 @@
         msg[d] = slots[d : d + 1, :]
 
     def packed(acc, plane, z):
-        return jnp.where((lane == 2 * z) | (lane == 2 * z + 1), roll(plane, 2 * z + 1, 1), acc)
+        return jnp.where(lane_pair == z, roll(plane, 2 * z + 1, 1), acc)
 
     def edges_of(s, _):
         load(0, t_h, tv, s).wait()
@@ -145,7 +148,7 @@
 
     lax.fori_loop(0, sources, edges_of, 0)
 
-    pl.semaphore_wait(barrier, devices - 1)
+    pl.semaphore_wait(barrier, len(others))
 
     def halo(k, s):
         def one(way, src, dst, dev):
@@ -183,15 +186,14 @@
 
     lax.fori_loop(0, sources, send_all, 0)
 
-    own = pltpu.make_async_copy(msg.at[me], box.at[me], st_recv)
+    pltpu.make_async_copy(msg.at[me], box.at[me], st_recv).start()
     for dx, dy in others:
-        ox_, oy_ = far(dx, dy)
+        to_x, to_y = far(dx, dy)
         pltpu.make_async_remote_copy(
-            src_ref=msg.at[ox_ * n_gy + oy_], dst_ref=box.at[me],
+            src_ref=msg.at[to_x * n_gy + to_y], dst_ref=box.at[me],
             send_sem=st_send, recv_sem=st_recv,
-            device_id=(ox_, oy_), device_id_type=MESH,
+            device_id=(to_x, to_y), device_id_type=MESH,
         ).start()
-    own.start()
 
     def coefficients(s, _):
         load(2, f_h, fv, s).wait()
@@ -269,45 +271,57 @@
 
     total[...] = jnp.zeros_like(total)
 
-    def sweep(k, src, dst, s):
+    group = 1
+
+    def sweep(k, src, dst, first):
         last = k == SWEEPS
-        arrive(k, s)
-        acc = jnp.zeros((rows_n, lanes_n), F32)
-        comb = jnp.where(odd, ix_hi[k, s], ix_lo[k, s])
-        below = None
-        a = src[s, 0]
+        members = [first * group + g for g in range(group)]
+        for s in members:
+            arrive(k, s)
+        packs = [jnp.zeros((rows_n, lanes_n), F32)] * group
+        combs = [jnp.where(odd, ix_hi[k, s], ix_lo[k, s]) for s in members]
+        belows = [None] * group
+        planes = [src[s, 0] for s in members]
         for z in range(levels):
-            above = src[s, z + 1] if z + 1 < levels else None
-            u = roll(comb, -(2 * z + 1), 1)
-            a_l = roll(jnp.where(last_lane, u, a), 1, 1)
-            a_r = roll(jnp.where(first_lane, u, a), -1, 1)
-            a_u = jnp.where(first_row, iy_lo[k, s, z : z + 1, :], roll(a, 1, 0))
-            a_d = jnp.where(last_row, iy_hi[k, s, z : z + 1, :], roll(a, -1, 0))
-            out = (sp[s, z] + c_l[s, z] * a_l) + (c_r[s, z] * a_r + c_u[s, z] * a_u)
-            out = out + c_d[s, z] * a_d
-            if below is not None:
-                out = out + c_b[s, z] * below
-            if above is not None:
-                out = out + c_t[s, z] * above
-            dst[s, z] = out
+            outs = []
+            for g, s in enumerate(members):
+                above = src[s, z + 1] if z + 1 < levels else None
+                a, below = planes[g], belows[g]
+                u = roll(combs[g], -(2 * z + 1), 1)
+                a_l = roll(jnp.where(last_lane, u, a), 1, 1)
+                a_r = roll(jnp.where(first_lane, u, a), -1, 1)
+                a_u = jnp.where(first_row, iy_lo[k, s, z : z + 1, :], roll(a, 1, 0))
+                a_d = jnp.where(last_row, iy_hi[k, s, z : z + 1, :], roll(a, -1, 0))
+                out = (sp[s, z] + c_l[s, z] * a_l) + (c_r[s, z] * a_r + c_u[s, z] * a_u)
+                out = out + c_d[s, z] * a_d
+                if below is not None:
+                    out = out + c_b[s, z] * below
+                if above is not None:
+                    out = out + c_t[s, z] * above
+                dst[s, z] = out
+                if not last:
+                    ry_hi[s, z : z + 1, :] = out[rows_n - 1 : rows_n]
+                    ry_lo[s, z : z + 1, :] = out[0:1]
+                    packs[g] = packed(packs[g], out, z)
+                outs.append(out)
+                belows[g], planes[g] = a, above
             if last:
-                total[z] = total[z] + out
-            else:
-                ry_hi[s, z : z + 1, :] = out[rows_n - 1 : rows_n]
-                ry_lo[s, z : z + 1, :] = out[0:1]
-                acc = packed(acc, out, z)
-            below, a = a, above
+                total[z] = total[z] + functools.reduce(jnp.add, outs)
         if not last:
-            oy_hi[k + 1, s] = ey_hi[s] * ry_hi[s]
-            oy_lo[k + 1, s] = ey_lo[s] * ry_lo[s]
-            ox[k + 1, s] = ex[s] * acc
-            send(k + 1, s)
+            for g, s in enumerate(members):
+                oy_hi[k + 1, s] = ey_hi[s] * ry_hi[s]
+                oy_lo[k + 1, s] = ey_lo[s] * ry_lo[s]
+                ox[k + 1, s] = ex[s] * packs[g]
+            for s in members:
+                send(k + 1, s)
         return 0
 
     held = (a0, adjv)
     for k in range(1, SWEEPS + 1):
         src, dst = held[(k - 1) % 2], held[k % 2]
-        lax.fori_loop(0, sources, lambda s, _, k=k, src=src, dst=dst: sweep(k, src, dst, s), 0)
+        lax.fori_loop(
+            0, sources // group, lambda i, _, k=k, src=src, dst=dst: sweep(k, src, dst, i), 0
+        )
 
     acc = jnp.zeros((rows_n, lanes_n), F32)
     for z in range(levels):
@@ -345,40 +359,44 @@
     lax.fori_loop(0, sources, drained, 0)
     rest = msg.at[pl.ds(0, devices - 1)]
     pltpu.make_async_copy(rest, rest, st_send).wait()
-    small[3].wait()
 
     for copy, _, takes in finals:
         @pl.when(takes)
         def _(copy=copy):
             copy.wait_recv()
 
-    comb = jnp.where(odd, tix_hi[...], tix_lo[...])
+    slow.wait()
+    rows_lo[...] = tiy_lo[...]
+    rows_hi[...] = tiy_hi[...]
+    columns[...] = jnp.where(odd, tix_hi[...], tix_lo[...])
+    for copy, sends, _ in finals:
+        @pl.when(sends)
+        def _(copy=copy):
+            copy.wait_send()
+
+
+def deliver(adj_v, total, rows_lo, rows_hi, columns, slv, adj_h, grad_h, gradv, sem):
+    whole = pltpu.make_async_copy(adj_v, adj_h, sem.at[0])
+    whole.start()
+    levels, rows_n, lanes_n = total.shape
+    sub = lax.broadcasted_iota(jnp.int32, (rows_n, lanes_n), 0)
+    lane = lax.broadcasted_iota(jnp.int32, (rows_n, lanes_n), 1)
+    comb = columns[...]
     for z in range(levels):
         cells = total[z]
         u = roll(comb, -(2 * z + 1), 1)
         beside = (
-            roll(jnp.where(last_lane, u, cells), 1, 1)
-            + roll(jnp.where(first_lane, u, cells), -1, 1)
+            roll(jnp.where(lane == lanes_n - 1, u, cells), 1, 1)
+            + roll(jnp.where(lane == 0, u, cells), -1, 1)
         ) + (
-            jnp.where(first_row, tiy_lo[z : z + 1, :], roll(cells, 1, 0))
-            + jnp.where(last_row, tiy_hi[z : z + 1, :], roll(cells, -1, 0))
+            jnp.where(sub == 0, rows_lo[z : z + 1, :], roll(cells, 1, 0))
+            + jnp.where(sub == rows_n - 1, rows_hi[z : z + 1, :], roll(cells, -1, 0))
         )
         gradv[z] = slv[z] * (cells + 0.125 * (beside - 4.0 * cells))
-    for copy, sends, _ in finals:
-        @pl.when(sends)
-        def _(copy=copy):
-            copy.wait_send()
-
-
-def deliver(adj_v, grad_v, adj_h, grad_h, sem):
-    copies = [
-        pltpu.make_async_copy(adj_v, adj_h, sem.at[0]),
-        pltpu.make_async_copy(grad_v, grad_h, sem.at[1]),
-    ]
-    for copy in copies:
-        copy.start()
-    for copy in copies:
-        copy.wait()
+    gradient = pltpu.make_async_copy(gradv, grad_h, sem.at[1])
+    gradient.start()
+    gradient.wait()
+    whole.wait()
 
 
 def shards(
@@ -404,18 +422,21 @@
     )
     results = pl.pallas_call(
         functools.partial(kernel, n_gx, n_gy),
-        out_shape=(
-            jax.ShapeDtypeStruct(traveltime.shape, F32),
-            jax.ShapeDtypeStruct(slowness.shape, F32),
-        ),
+        out_shape=[
+            jax.ShapeDtypeStruct(shape, F32)
+            for shape in (
+                traveltime.shape, slowness.shape, (levels, lanes_n), (levels, lanes_n),
+                (rows_n, lanes_n), slowness.shape,
+            )
+        ],
         in_specs=[pl.BlockSpec(memory_space=pltpu.HBM)] * 7,
-        out_specs=[pl.BlockSpec(memory_space=pltpu.VMEM)] * 2,
+        out_specs=[pl.BlockSpec(memory_space=pltpu.VMEM)] * 6,
         scratch_shapes=[
-            big, pltpu.VMEM(traveltime.shape, jnp.int32), big, flat,
+            big, pltpu.VMEM(traveltime.shape, jnp.int32), big,
             pltpu.VMEM((sources, count), F32),
             pltpu.VMEM((1, count), jnp.int32),
             pltpu.VMEM((1, count), jnp.int32),
-            big, big, big, big, big, big, big, flat,
+            big, big, big, big, big, big, big,
             pltpu.VMEM((lanes_n, count), F32),
             pltpu.VMEM((devices, 1, lanes_n), F32),
             pltpu.VMEM((devices, 1, lanes_n), F32),
@@ -437,9 +458,9 @@
             jax.ShapeDtypeStruct(traveltime.shape, F32),
             jax.ShapeDtypeStruct(slowness.shape, F32),
         ),
-        in_specs=[pl.BlockSpec(memory_space=pltpu.VMEM)] * 2,
+        in_specs=[pl.BlockSpec(memory_space=pltpu.VMEM)] * 6,
         out_specs=[pl.BlockSpec(memory_space=pltpu.HBM)] * 2,
-        scratch_shapes=[dma((2,))],
+        scratch_shapes=[flat, dma((2,))],
         compiler_params=pltpu.CompilerParams(vmem_limit_bytes=4 * 1024 * 1024),
         name="deliver",
     )(*results)

time: 30.5 us -> 30.4 us (level)
  no operation moved by 1% of the time
where the time goes in v3:
time: 30.4 us; the launch traced here: 30.2 us
  Pallas kernels  29.6 us (97%)
  between operations  0.64 us (2%)
    pallas_call x1, Pallas kernels, shards(): pl.pallas_call(functools.partial(kernel, n_gx, n_gy), out_shape=[jax.Shap...  28.5 us
    pallas_call x1, Pallas kernels, shards(): pl.pallas_call(deliver, out_shape=(jax.ShapeDtypeStruct(traveltime.shape,...  1.05 us

profile of v3, /device:TPU:0, one launch (start us, length us, event | category | flops | bytes accessed | tf_op | source)
XLA Modules:
  0.0 30.2 jit_solution(3193751762390830926)
XLA Ops:
  0.6 28.5 %tomography.1 = (f32[8,32,8,128]{3,2,1,0:T(8,128)S(1)}, f32[32,8,128]{2,1,0:T(8,128)S(1)}, f32[32,128]{1,0:T(8,128)S(1)}, f32[32,128]{1,0:T(8,128)S(1)}, f32[8,1...) custom-call(f32[8,32,8,128]{3,2,1,0:T(8,128)} %t_h.1, f32[8,32,8,128]{3,2,1,0:T(8,128)} %a_h.1, s32[8,32,8,128]{3,2,1,0:T(8,128)} %f_h.1, ...), custom_call_target="tpu_custom_call" | custom-call | tf_op jit(solution)/shard_map/tomography/pallas_call | solution.py:423
  29.2 1.0 %deliver.1 = (f32[8,32,8,128]{3,2,1,0:T(8,128)}, f32[32,8,128]{2,1,0:T(8,128)}) custom-call(f32[8,32,8,128]{3,2,1,0:T(8,128)S(1)} %get-tuple-element.8.adj_v, f32[32,8,128]{2,1,0:T(8,128)S(1)} %get-tuple-element.9.total, f32[32,128]{1,0:T(8,128)S(1)} %get-tuple-element.10.rows_lo, f32[32,128]{1,0:T(8,128)S(1)} %get-tuple-element.11.rows_hi, ...), custom_call_target="tpu_custom_call" | custom-call | tf_op jit(solution)/shard_map/deliver/pallas_call | solution.py:455
